TPU v7x, 32 devices: a whole 2x2x4 slice. The times are simulated.
32 devices in a mesh: ctxa: 4 (over z), ctxb: 8 (over y, x, core).
Axes of the slice: x: 2, y: 2, z: 4, core: 2. Of those that a mesh axis runs over, the one named last changes fastest.
Arguments:
- queries: bfloat16 [8192, 8, 128], P(('ctxa', 'ctxb')), may hold values from -14 to 14
- key_vectors: bfloat16 [8192, 128], P(('ctxa', 'ctxb')), may hold values from -5 to 5
- value_vectors: bfloat16 [8192, 128], P(('ctxa', 'ctxb')), may hold values from -12 to 12
- out_grad: bfloat16 [8192, 8, 128], P(('ctxa', 'ctxb')), may hold values from -6 to 6
Outputs:
- attention: bfloat16 [8192, 8, 128], P(('ctxa', 'ctxb'))
- query_grad: bfloat16 [8192, 8, 128], P(('ctxa', 'ctxb'))
- key_grad: bfloat16 [8192, 128], P(('ctxa', 'ctxb'))
- value_grad: bfloat16 [8192, 128], P(('ctxa', 'ctxb'))
All inputs are finite; a program needn't handle non-finite values.
Results may differ from a plain program's by a relative error of at most 0.012.
Values may be sent and summed in bfloat16 or wider, within the bound.
No kernel may reach another device: no remote copies, remote signals or barrier semaphores. Data moves between devices by JAX's collectives and lax.ppermute only.
A program may use at most 64 MiB of HBM per device.

v0:
```python
import jax
import jax.numpy as jnp
from jax import lax
from jax.sharding import PartitionSpec as P

BLK = 128
WIN = 1024
FAR = 6


def shifted(value, axis, by):
    count = lax.axis_size(axis)
    pairs = [(i, i + by) for i in range(count) if 0 <= i + by < count]
    return lax.ppermute(value, axis, pairs)


def body(queries, key_vectors, value_vectors, out_grad):
    tok_count = key_vectors.shape[0]
    heads = queries.shape[1]
    width = key_vectors.shape[1]
    score_scale = 1.0 / width**0.5
    inner_size = lax.axis_size("ctxb")
    devices_all = lax.axis_size("ctxa") * inner_size
    device = lax.axis_index("ctxa") * inner_size + lax.axis_index("ctxb")
    start_pos = device * tok_count
    shards = WIN // tok_count
    stride = 2 * WIN // BLK
    half_block = BLK // 2
    key_span = WIN + BLK
    paired = jnp.stack([key_vectors, value_vectors])
    pieces = []
    for behind in range(shards, 0, -1):
        pieces.append(shifted(paired, ("ctxa", "ctxb"), behind))
    window_pairs = jnp.concatenate(pieces + [paired], axis=1)
    distances = []
    far_list = []
    for level_index in range(FAR):
        distance = stride * 2**level_index * BLK // tok_count
        if distance < devices_all:
            far_list.append(shifted(paired, ("ctxa", "ctxb"), distance))
            distances.append(distance)
    level_count = len(distances)
    far_pairs = jnp.stack(far_list, axis=1)
    far_valid = jnp.stack([device >= distance for distance in distances])
    far_keys = level_count * BLK
    total_keys = key_span + far_keys
    offsets = jnp.arange(key_span, dtype=jnp.int32)
    inside = jnp.arange(half_block, dtype=jnp.int32)
    far_mask = jnp.broadcast_to(jnp.repeat(far_valid, BLK)[None, :], (half_block, far_keys))
    row_count = half_block * heads

    def sub_block(block_index, running):
        attention, query_grad, window_grad, far_grad = running
        first_row = block_index * half_block
        key_start = first_row // BLK * BLK
        window_part = lax.dynamic_slice_in_dim(window_pairs, key_start, key_span, 1)
        far_part = lax.dynamic_slice_in_dim(far_pairs, key_start, BLK, 2).reshape(
            2, far_keys, width
        )
        key_rows = jnp.concatenate([window_part[0], far_part[0]], axis=0)
        value_rows = jnp.concatenate([window_part[1], far_part[1]], axis=0)
        q_pos = start_pos + first_row + inside
        k_pos = start_pos - WIN + key_start + offsets
        near_mask = (
            (k_pos[None, :] > q_pos[:, None] - WIN)
            & (k_pos[None, :] <= q_pos[:, None])
            & (k_pos[None, :] >= 0)
        )
        visible = jnp.concatenate([near_mask, far_mask], axis=1)
        visible = jnp.broadcast_to(visible[:, None, :], (half_block, heads, total_keys)).reshape(
            row_count, total_keys
        )
        q_rows = lax.dynamic_slice_in_dim(queries, first_row, half_block, 0).reshape(
            row_count, width
        )
        grad_rows = lax.dynamic_slice_in_dim(out_grad, first_row, half_block, 0).reshape(
            row_count, width
        )
        scores = (
            jnp.einsum("rd,kd->rk", q_rows, key_rows, preferred_element_type=jnp.float32)
            * score_scale
        )
        scores = jnp.where(visible, scores, -jnp.inf)
        row_max = jnp.max(scores, axis=1, keepdims=True)
        log_total = row_max + jnp.log(jnp.sum(jnp.exp(scores - row_max), axis=1, keepdims=True))
        probs = jnp.exp(scores - log_total)
        probs_low = probs.astype(jnp.bfloat16)
        out_rows = jnp.dot(probs_low, value_rows, preferred_element_type=jnp.float32).astype(
            jnp.bfloat16
        )
        row_delta = jnp.sum(
            grad_rows.astype(jnp.float32) * out_rows.astype(jnp.float32), axis=1, keepdims=True
        )
        prob_grad = jnp.einsum(
            "rd,kd->rk", grad_rows, value_rows, preferred_element_type=jnp.float32
        )
        score_grad = (probs * (prob_grad - row_delta)).astype(jnp.bfloat16)
        q_grad_rows = (
            jnp.dot(score_grad, key_rows, preferred_element_type=jnp.float32) * score_scale
        ).astype(jnp.bfloat16)
        key_terms = (
            jnp.einsum("rk,rd->kd", score_grad, q_rows, preferred_element_type=jnp.float32)
            * score_scale
        )
        value_terms = jnp.einsum(
            "rk,rd->kd", probs_low, grad_rows, preferred_element_type=jnp.float32
        )
        grad_terms = jnp.stack([key_terms, value_terms])
        previous = lax.dynamic_slice_in_dim(window_grad, key_start, key_span, 1)
        window_grad = lax.dynamic_update_slice_in_dim(
            window_grad, previous + grad_terms[:, :key_span], key_start, 1
        )
        far_terms = grad_terms[:, key_span:].reshape(2, level_count, BLK, width)
        previous_far = lax.dynamic_slice_in_dim(far_grad, key_start, BLK, 2)
        far_grad = lax.dynamic_update_slice_in_dim(far_grad, previous_far + far_terms, key_start, 2)
        attention = lax.dynamic_update_slice_in_dim(
            attention, out_rows.reshape(half_block, heads, width), first_row, 0
        )
        query_grad = lax.dynamic_update_slice_in_dim(
            query_grad, q_grad_rows.reshape(half_block, heads, width), first_row, 0
        )
        return (attention, query_grad, window_grad, far_grad)

    running = (
        jnp.zeros((tok_count, heads, width), jnp.bfloat16),
        jnp.zeros((tok_count, heads, width), jnp.bfloat16),
        jnp.zeros((2, WIN + tok_count, width), jnp.float32),
        jnp.zeros((2, level_count, tok_count, width), jnp.float32),
    )
    attention, query_grad, window_grad, far_grad = lax.fori_loop(
        0, tok_count // half_block, sub_block, running
    )
    own_grad = window_grad[:, shards * tok_count :]
    for behind in range(1, shards + 1):
        piece = window_grad[:, (shards - behind) * tok_count : (shards - behind + 1) * tok_count]
        own_grad = own_grad + shifted(piece, ("ctxa", "ctxb"), -behind)
    for level_index, distance in enumerate(distances):
        own_grad = own_grad + shifted(far_grad[:, level_index], ("ctxa", "ctxb"), -distance)
    return (
        attention,
        query_grad,
        own_grad[0].astype(jnp.bfloat16),
        own_grad[1].astype(jnp.bfloat16),
    )


def solution(mesh):
    in_specs = (
        P(("ctxa", "ctxb"), None, None),
        P(("ctxa", "ctxb"), None),
        P(("ctxa", "ctxb"), None),
        P(("ctxa", "ctxb"), None, None),
    )
    out_specs = (
        P(("ctxa", "ctxb"), None, None),
        P(("ctxa", "ctxb"), None, None),
        P(("ctxa", "ctxb"), None),
        P(("ctxa", "ctxb"), None),
    )
    return jax.shard_map(body, mesh=mesh, in_specs=in_specs, out_specs=out_specs, check_vma=False)
```

profile of v0, /device:TPU:15, one launch (start us, length us, event | category | flops | bytes accessed | tf_op | source)
XLA Modules:
  0.0 103.9 jit_solution(2559279426059569024)
XLA Ops:
  1.5 3.1 %collective-permute-start = (bf16[2,256,128]{2,1,0:T(8,128)(2,1)S(1)}, bf16[2,256,128]{2,1,0:T(8,128)(2,1)S(1)}, u32[]{:S(2)}, u32[]{:S(2)}) collective-permute-start(bf16[2,256,128]{2,1,0:T(8,128)(2,1)S(1)} %pad_maximum_fusion.8), channel_id=1, source_target_pairs={{0,4},{1,5},{2,6},{3,7},{4,8},{5,9},{6,10},{7,11},{8,12},{9,13},{1... | collective-permute-start | bytes 393224 | tf_op jit(solution)/shard_map/ppermute | solution.py:14
  4.7 4.0 %collective-permute-start.1 = (bf16[2,256,128]{2,1,0:T(8,128)(2,1)S(1)}, bf16[2,256,128]{2,1,0:T(8,128)(2,1)S(1)}, u32[]{:S(2)}, u32[]{:S(2)}) collective-permute-start(bf16[2,256,128]{2,1,0:T(8,128)(2,1)S(1)} %pad_maximum_fusion.8), channel_id=1, source_target_pairs={{0,3},{1,4},{2,5},{3,6},{4,7},{5,8},{6,9},{7,10},{8,11},{9,12},{10... | collective-permute-start | bytes 393224 | tf_op jit(solution)/shard_map/ppermute | solution.py:14
  8.7 3.1 %collective-permute-start.2 = (bf16[2,256,128]{2,1,0:T(8,128)(2,1)S(1)}, bf16[2,256,128]{2,1,0:T(8,128)(2,1)S(1)}, u32[]{:S(2)}, u32[]{:S(2)}) collective-permute-start(bf16[2,256,128]{2,1,0:T(8,128)(2,1)S(1)} %pad_maximum_fusion.8), channel_id=1, source_target_pairs={{0,2},{1,3},{2,4},{3,5},{4,6},{5,7},{6,8},{7,9},{8,10},{9,11},{10,... | collective-permute-start | bytes 393224 | tf_op jit(solution)/shard_map/ppermute | solution.py:14
  11.8 2.8 %collective-permute-start.3 = (bf16[2,256,128]{2,1,0:T(8,128)(2,1)S(1)}, bf16[2,256,128]{2,1,0:T(8,128)(2,1)S(1)}, u32[]{:S(2)}, u32[]{:S(2)}) collective-permute-start(bf16[2,256,128]{2,1,0:T(8,128)(2,1)S(1)} %pad_maximum_fusion.8), channel_id=1, source_target_pairs={{0,1},{1,2},{2,3},{3,4},{4,5},{5,6},{6,7},{7,8},{8,9},{9,10},{10,1... | collective-permute-start | bytes 393224 | tf_op jit(solution)/shard_map/ppermute | solution.py:14
  16.1 2.6 %collective-permute-start.4 = (bf16[2,256,128]{2,1,0:T(8,128)(2,1)S(1)}, bf16[2,256,128]{2,1,0:T(8,128)(2,1)S(1)}, u32[]{:S(2)}, u32[]{:S(2)}) collective-permute-start(bf16[2,256,128]{2,1,0:T(8,128)(2,1)S(1)} %pad_maximum_fusion.8), channel_id=1, source_target_pairs={{0,8},{1,9},{2,10},{3,11},{4,12},{5,13},{6,14},{7,15},{8,16},{9,17... | collective-permute-start | bytes 393224 | tf_op jit(solution)/shard_map/ppermute | solution.py:14
  19.7 2.8 %collective-permute-done.5 = bf16[2,256,128]{2,1,0:T(8,128)(2,1)S(1)} collective-permute-done((bf16[2,256,128]{2,1,0:T(8,128)(2,1)S(1)}, bf16[2,256,128]{2,1,0:T(8,128)(2,1)S(1)}, u32[]{:S(2)}, u32[]{:S(2)}) %collective-permute-start.5) | collective-permute-done | bytes 131104 | tf_op jit(solution)/shard_map/ppermute | solution.py:14
  22.4 2.8 %collective-permute-done.4 = bf16[2,256,128]{2,1,0:T(8,128)(2,1)S(1)} collective-permute-done((bf16[2,256,128]{2,1,0:T(8,128)(2,1)S(1)}, bf16[2,256,128]{2,1,0:T(8,128)(2,1)S(1)}, u32[]{:S(2)}, u32[]{:S(2)}) %collective-permute-start.4) | collective-permute-done | bytes 131104 | tf_op jit(solution)/shard_map/ppermute | solution.py:14
  27.1 34.9 %while.23 = (s32[]{:T(128)}, bf16[256,8,128]{2,1,0:T(8,128)(2,1)}, bf16[256,8,128]{2,1,0:T(8,128)(2,1)}, f32[2,1280,128]{2,1,0:T(8,128)S(1)}, f32[2,2,256,128]{3...) while((s32[]{:T(128)}, bf16[256,8,128]{2,1,0:T(8,128)(2,1)}, ...), condition=%wide.region_4.5_spmd.clone, body=%wide.region_0.4_spmd.clone.sunk | while | flops 1121298944 | bytes 33004372 | solution.py:130
  27.5 1.8 %fusion.56 = (f32[512]{0:T(512)S(1)}, f32[512,1408]{1,0:T(8,128)S(1)}) fusion(bf16[256,128]{1,0:T(8,128)(2,1)S(1)} %bitcast.85, bf16[1152,128]{1,0:T(8,128)(2,1)S(1)} %get-tuple-element.522, bf16[256,8,128]{2,1,0:T(8,128)(2,1)} %get-tuple-element.582, s32[]{:T(128)S(6)} %select_n.75, pred[64,1408]{1,0:T(8,128)(4,1)S(1)} %pad_add_fusion.3), kind=kOutput, calls=%fused_computation.73.clone.1 | convolution fusion | flops 187432448 | bytes 3467268 | tf_op jit(solution)/shard_map/while/body/eval_jaxpr/rd,kd->rk/dot_general | solution.py:80
  36.3 1.8 %fusion.56 = (f32[512]{0:T(512)S(1)}, f32[512,1408]{1,0:T(8,128)S(1)}) fusion(bf16[256,128]{1,0:T(8,128)(2,1)S(1)} %bitcast.85, bf16[1152,128]{1,0:T(8,128)(2,1)S(1)} %get-tuple-element.522, bf16[256,8,128]{2,1,0:T(8,128)(2,1)} %get-tuple-element.582, s32[]{:T(128)S(6)} %select_n.75, pred[64,1408]{1,0:T(8,128)(4,1)S(1)} %pad_add_fusion.3), kind=kOutput, calls=%fused_computation.73.clone.1 | convolution fusion | flops 187432448 | bytes 3467268 | tf_op jit(solution)/shard_map/while/body/eval_jaxpr/rd,kd->rk/dot_general | solution.py:80
  42.0 1.5 %fusion.59 = f32[1,1408,128]{2,1,0:T(8,128)S(1)} fusion(bf16[512,1408]{1,0:T(8,128)(2,1)S(1)} %fusion.57, bf16[256,8,128]{2,1,0:T(8,128)(2,1)} %get-tuple-element.582, s32[]{:T(128)S(6)} %select_n.75), kind=kOutput, calls=%fused_computation.12.clone.1 | convolution fusion | flops 184729600 | bytes 2293764 | tf_op jit(solution)/shard_map/while/body/eval_jaxpr/rk,rd->kd/dot_general | solution.py:102
  45.0 1.8 %fusion.56 = (f32[512]{0:T(512)S(1)}, f32[512,1408]{1,0:T(8,128)S(1)}) fusion(bf16[256,128]{1,0:T(8,128)(2,1)S(1)} %bitcast.85, bf16[1152,128]{1,0:T(8,128)(2,1)S(1)} %get-tuple-element.522, bf16[256,8,128]{2,1,0:T(8,128)(2,1)} %get-tuple-element.582, s32[]{:T(128)S(6)} %select_n.75, pred[64,1408]{1,0:T(8,128)(4,1)S(1)} %pad_add_fusion.3), kind=kOutput, calls=%fused_computation.73.clone.1 | convolution fusion | flops 187432448 | bytes 3467268 | tf_op jit(solution)/shard_map/while/body/eval_jaxpr/rd,kd->rk/dot_general | solution.py:80
  50.8 1.5 %fusion.59 = f32[1,1408,128]{2,1,0:T(8,128)S(1)} fusion(bf16[512,1408]{1,0:T(8,128)(2,1)S(1)} %fusion.57, bf16[256,8,128]{2,1,0:T(8,128)(2,1)} %get-tuple-element.582, s32[]{:T(128)S(6)} %select_n.75), kind=kOutput, calls=%fused_computation.12.clone.1 | convolution fusion | flops 184729600 | bytes 2293764 | tf_op jit(solution)/shard_map/while/body/eval_jaxpr/rk,rd->kd/dot_general | solution.py:102
  53.7 1.8 %fusion.56 = (f32[512]{0:T(512)S(1)}, f32[512,1408]{1,0:T(8,128)S(1)}) fusion(bf16[256,128]{1,0:T(8,128)(2,1)S(1)} %bitcast.85, bf16[1152,128]{1,0:T(8,128)(2,1)S(1)} %get-tuple-element.522, bf16[256,8,128]{2,1,0:T(8,128)(2,1)} %get-tuple-element.582, s32[]{:T(128)S(6)} %select_n.75, pred[64,1408]{1,0:T(8,128)(4,1)S(1)} %pad_add_fusion.3), kind=kOutput, calls=%fused_computation.73.clone.1 | convolution fusion | flops 187432448 | bytes 3467268 | tf_op jit(solution)/shard_map/while/body/eval_jaxpr/rd,kd->rk/dot_general | solution.py:80
  63.4 1.9 %collective-permute-start.10 = (f32[2,256,128]{2,1,0:T(8,128)S(1)}, f32[2,256,128]{2,1,0:T(8,128)S(1)}, u32[]{:S(2)}, u32[]{:S(2)}) collective-permute-start(f32[2,256,128]{2,1,0:T(8,128)S(1)} %get-tuple-element.432), channel_id=1, source_target_pairs={{8,0},{9,1},{10,2},{11,3},{12,4},{13,5},{14,6},{15,7},{16,8},{17,9... | collective-permute-start | bytes 786440 | tf_op jit(solution)/shard_map/ppermute | solution.py:14
  65.4 2.7 %collective-permute-start.9 = (f32[2,256,128]{2,1,0:T(8,128)S(1)}, f32[2,256,128]{2,1,0:T(8,128)S(1)}, u32[]{:S(2)}, u32[]{:S(2)}) collective-permute-start(f32[2,256,128]{2,1,0:T(8,128)S(1)} %get-tuple-element.431), channel_id=1, source_target_pairs={{4,0},{5,1},{6,2},{7,3},{8,4},{9,5},{10,6},{11,7},{12,8},{13,9},{1... | collective-permute-start | bytes 786440 | tf_op jit(solution)/shard_map/ppermute | solution.py:14
  68.2 2.8 %collective-permute-start.8 = (f32[2,256,128]{2,1,0:T(8,128)S(1)}, f32[2,256,128]{2,1,0:T(8,128)S(1)}, u32[]{:S(2)}, u32[]{:S(2)}) collective-permute-start(f32[2,256,128]{2,1,0:T(8,128)S(1)} %get-tuple-element.429), channel_id=1, source_target_pairs={{3,0},{4,1},{5,2},{6,3},{7,4},{8,5},{9,6},{10,7},{11,8},{12,9},{13... | collective-permute-start | bytes 786440 | tf_op jit(solution)/shard_map/ppermute | solution.py:14
  71.0 2.6 %collective-permute-start.7 = (f32[2,256,128]{2,1,0:T(8,128)S(1)}, f32[2,256,128]{2,1,0:T(8,128)S(1)}, u32[]{:S(2)}, u32[]{:S(2)}) collective-permute-start(f32[2,256,128]{2,1,0:T(8,128)S(1)} %get-tuple-element.430), channel_id=1, source_target_pairs={{2,0},{3,1},{4,2},{5,3},{6,4},{7,5},{8,6},{9,7},{10,8},{11,9},{12,... | collective-permute-start | bytes 786440 | tf_op jit(solution)/shard_map/ppermute | solution.py:14
  73.6 2.9 %collective-permute-start.6 = (f32[2,256,128]{2,1,0:T(8,128)S(1)}, f32[2,256,128]{2,1,0:T(8,128)S(1)}, u32[]{:S(2)}, u32[]{:S(2)}) collective-permute-start(f32[2,256,128]{2,1,0:T(8,128)S(1)} %get-tuple-element.428), channel_id=1, source_target_pairs={{1,0},{2,1},{3,2},{4,3},{5,4},{6,5},{7,6},{8,7},{9,8},{10,9},{11,1... | collective-permute-start | bytes 786440 | tf_op jit(solution)/shard_map/ppermute | solution.py:14
  76.5 6.1 %collective-permute-done.10 = f32[2,256,128]{2,1,0:T(8,128)S(1)} collective-permute-done((f32[2,256,128]{2,1,0:T(8,128)S(1)}, f32[2,256,128]{2,1,0:T(8,128)S(1)}, u32[]{:S(2)}, u32[]{:S(2)}) %collective-permute-start.10) | collective-permute-done | bytes 262176 | tf_op jit(solution)/shard_map/ppermute | solution.py:14
  82.6 5.6 %collective-permute-done.9 = f32[2,256,128]{2,1,0:T(8,128)S(1)} collective-permute-done((f32[2,256,128]{2,1,0:T(8,128)S(1)}, f32[2,256,128]{2,1,0:T(8,128)S(1)}, u32[]{:S(2)}, u32[]{:S(2)}) %collective-permute-start.9) | collective-permute-done | bytes 262176 | tf_op jit(solution)/shard_map/ppermute | solution.py:14
  88.1 5.9 %collective-permute-done.8 = f32[2,256,128]{2,1,0:T(8,128)S(1)} collective-permute-done((f32[2,256,128]{2,1,0:T(8,128)S(1)}, f32[2,256,128]{2,1,0:T(8,128)S(1)}, u32[]{:S(2)}, u32[]{:S(2)}) %collective-permute-start.8) | collective-permute-done | bytes 262176 | tf_op jit(solution)/shard_map/ppermute | solution.py:14
  94.0 5.4 %collective-permute-done.7 = f32[2,256,128]{2,1,0:T(8,128)S(1)} collective-permute-done((f32[2,256,128]{2,1,0:T(8,128)S(1)}, f32[2,256,128]{2,1,0:T(8,128)S(1)}, u32[]{:S(2)}, u32[]{:S(2)}) %collective-permute-start.7) | collective-permute-done | bytes 262176 | tf_op jit(solution)/shard_map/ppermute | solution.py:14
  99.4 3.7 %collective-permute-done.6 = f32[2,256,128]{2,1,0:T(8,128)S(1)} collective-permute-done((f32[2,256,128]{2,1,0:T(8,128)S(1)}, f32[2,256,128]{2,1,0:T(8,128)S(1)}, u32[]{:S(2)}, u32[]{:S(2)}) %collective-permute-start.6) | collective-permute-done | bytes 262176 | tf_op jit(solution)/shard_map/ppermute | solution.py:14
  (106 shorter events, 31.5 us)
Async XLA Ops:
  1.5 14.6 %collective-permute-start = (bf16[2,256,128]{2,1,0:T(8,128)(2,1)S(1)}, bf16[2,256,128]{2,1,0:T(8,128)(2,1)S(1)}, u32[]{:S(2)}, u32[]{:S(2)}) collective-permute-start(bf16[2,256,128]{2,1,0:T(8,128)(2,1)S(1)} %pad_maximum_fusion.8), channel_id=1, source_target_pairs={{0,4},{1,5},{2,6},{3,7},{4,8},{5,9},{6,10},{7,11},{8,12},{9,13},{1... | collective-permute-start | bytes 393224 | tf_op jit(solution)/shard_map/ppermute | solution.py:14
  4.7 14.0 %collective-permute-start.1 = (bf16[2,256,128]{2,1,0:T(8,128)(2,1)S(1)}, bf16[2,256,128]{2,1,0:T(8,128)(2,1)S(1)}, u32[]{:S(2)}, u32[]{:S(2)}) collective-permute-start(bf16[2,256,128]{2,1,0:T(8,128)(2,1)S(1)} %pad_maximum_fusion.8), channel_id=1, source_target_pairs={{0,3},{1,4},{2,5},{3,6},{4,7},{5,8},{6,9},{7,10},{8,11},{9,12},{10... | collective-permute-start | bytes 393224 | tf_op jit(solution)/shard_map/ppermute | solution.py:14
  8.7 10.0 %collective-permute-start.2 = (bf16[2,256,128]{2,1,0:T(8,128)(2,1)S(1)}, bf16[2,256,128]{2,1,0:T(8,128)(2,1)S(1)}, u32[]{:S(2)}, u32[]{:S(2)}) collective-permute-start(bf16[2,256,128]{2,1,0:T(8,128)(2,1)S(1)} %pad_maximum_fusion.8), channel_id=1, source_target_pairs={{0,2},{1,3},{2,4},{3,5},{4,6},{5,7},{6,8},{7,9},{8,10},{9,11},{10,... | collective-permute-start | bytes 393224 | tf_op jit(solution)/shard_map/ppermute | solution.py:14
  11.8 6.9 %collective-permute-start.3 = (bf16[2,256,128]{2,1,0:T(8,128)(2,1)S(1)}, bf16[2,256,128]{2,1,0:T(8,128)(2,1)S(1)}, u32[]{:S(2)}, u32[]{:S(2)}) collective-permute-start(bf16[2,256,128]{2,1,0:T(8,128)(2,1)S(1)} %pad_maximum_fusion.8), channel_id=1, source_target_pairs={{0,1},{1,2},{2,3},{3,4},{4,5},{5,6},{6,7},{7,8},{8,9},{9,10},{10,1... | collective-permute-start | bytes 393224 | tf_op jit(solution)/shard_map/ppermute | solution.py:14
  14.6 7.8 %collective-permute-start.5 = (bf16[2,256,128]{2,1,0:T(8,128)(2,1)S(1)}, bf16[2,256,128]{2,1,0:T(8,128)(2,1)S(1)}, u32[]{:S(2)}, u32[]{:S(2)}) collective-permute-start(bf16[2,256,128]{2,1,0:T(8,128)(2,1)S(1)} %pad_maximum_fusion.8), channel_id=1, source_target_pairs={{0,16},{1,17},{2,18},{3,19},{4,20},{5,21},{6,22},{7,23},{8,24},{9,... | collective-permute-start | bytes 393224 | tf_op jit(solution)/shard_map/ppermute | solution.py:14
  16.1 9.2 %collective-permute-start.4 = (bf16[2,256,128]{2,1,0:T(8,128)(2,1)S(1)}, bf16[2,256,128]{2,1,0:T(8,128)(2,1)S(1)}, u32[]{:S(2)}, u32[]{:S(2)}) collective-permute-start(bf16[2,256,128]{2,1,0:T(8,128)(2,1)S(1)} %pad_maximum_fusion.8), channel_id=1, source_target_pairs={{0,8},{1,9},{2,10},{3,11},{4,12},{5,13},{6,14},{7,15},{8,16},{9,17... | collective-permute-start | bytes 393224 | tf_op jit(solution)/shard_map/ppermute | solution.py:14
  29.3 1.8 %copy-start = (bf16[256,8,128]{2,1,0:T(8,128)(2,1)S(1)}, bf16[256,8,128]{2,1,0:T(8,128)(2,1)}, u32[]{:S(2)}) copy-start(bf16[256,8,128]{2,1,0:T(8,128)(2,1)} %get-tuple-element.585) | copy-start | bytes 1572868 | tf_op jit(solution)/shard_map/while
  38.1 1.8 %copy-start = (bf16[256,8,128]{2,1,0:T(8,128)(2,1)S(1)}, bf16[256,8,128]{2,1,0:T(8,128)(2,1)}, u32[]{:S(2)}) copy-start(bf16[256,8,128]{2,1,0:T(8,128)(2,1)} %get-tuple-element.585) | copy-start | bytes 1572868 | tf_op jit(solution)/shard_map/while
  46.8 1.8 %copy-start = (bf16[256,8,128]{2,1,0:T(8,128)(2,1)S(1)}, bf16[256,8,128]{2,1,0:T(8,128)(2,1)}, u32[]{:S(2)}) copy-start(bf16[256,8,128]{2,1,0:T(8,128)(2,1)} %get-tuple-element.585) | copy-start | bytes 1572868 | tf_op jit(solution)/shard_map/while
  55.5 1.8 %copy-start = (bf16[256,8,128]{2,1,0:T(8,128)(2,1)S(1)}, bf16[256,8,128]{2,1,0:T(8,128)(2,1)}, u32[]{:S(2)}) copy-start(bf16[256,8,128]{2,1,0:T(8,128)(2,1)} %get-tuple-element.585) | copy-start | bytes 1572868 | tf_op jit(solution)/shard_map/while
  62.1 11.4 %collective-permute-start.11 = (f32[2,256,128]{2,1,0:T(8,128)S(1)}, f32[2,256,128]{2,1,0:T(8,128)S(1)}, u32[]{:S(2)}, u32[]{:S(2)}) collective-permute-start(f32[2,256,128]{2,1,0:T(8,128)S(1)} %get-tuple-element.433), channel_id=1, source_target_pairs={{16,0},{17,1},{18,2},{19,3},{20,4},{21,5},{22,6},{23,7},{24,8},{25... | collective-permute-start | bytes 786440 | tf_op jit(solution)/shard_map/ppermute | solution.py:14
  63.4 19.1 %collective-permute-start.10 = (f32[2,256,128]{2,1,0:T(8,128)S(1)}, f32[2,256,128]{2,1,0:T(8,128)S(1)}, u32[]{:S(2)}, u32[]{:S(2)}) collective-permute-start(f32[2,256,128]{2,1,0:T(8,128)S(1)} %get-tuple-element.432), channel_id=1, source_target_pairs={{8,0},{9,1},{10,2},{11,3},{12,4},{13,5},{14,6},{15,7},{16,8},{17,9... | collective-permute-start | bytes 786440 | tf_op jit(solution)/shard_map/ppermute | solution.py:14
  65.4 22.7 %collective-permute-start.9 = (f32[2,256,128]{2,1,0:T(8,128)S(1)}, f32[2,256,128]{2,1,0:T(8,128)S(1)}, u32[]{:S(2)}, u32[]{:S(2)}) collective-permute-start(f32[2,256,128]{2,1,0:T(8,128)S(1)} %get-tuple-element.431), channel_id=1, source_target_pairs={{4,0},{5,1},{6,2},{7,3},{8,4},{9,5},{10,6},{11,7},{12,8},{13,9},{1... | collective-permute-start | bytes 786440 | tf_op jit(solution)/shard_map/ppermute | solution.py:14
  68.2 25.9 %collective-permute-start.8 = (f32[2,256,128]{2,1,0:T(8,128)S(1)}, f32[2,256,128]{2,1,0:T(8,128)S(1)}, u32[]{:S(2)}, u32[]{:S(2)}) collective-permute-start(f32[2,256,128]{2,1,0:T(8,128)S(1)} %get-tuple-element.429), channel_id=1, source_target_pairs={{3,0},{4,1},{5,2},{6,3},{7,4},{8,5},{9,6},{10,7},{11,8},{12,9},{13... | collective-permute-start | bytes 786440 | tf_op jit(solution)/shard_map/ppermute | solution.py:14
  71.0 28.4 %collective-permute-start.7 = (f32[2,256,128]{2,1,0:T(8,128)S(1)}, f32[2,256,128]{2,1,0:T(8,128)S(1)}, u32[]{:S(2)}, u32[]{:S(2)}) collective-permute-start(f32[2,256,128]{2,1,0:T(8,128)S(1)} %get-tuple-element.430), channel_id=1, source_target_pairs={{2,0},{3,1},{4,2},{5,3},{6,4},{7,5},{8,6},{9,7},{10,8},{11,9},{12,... | collective-permute-start | bytes 786440 | tf_op jit(solution)/shard_map/ppermute | solution.py:14
  73.6 29.5 %collective-permute-start.6 = (f32[2,256,128]{2,1,0:T(8,128)S(1)}, f32[2,256,128]{2,1,0:T(8,128)S(1)}, u32[]{:S(2)}, u32[]{:S(2)}) collective-permute-start(f32[2,256,128]{2,1,0:T(8,128)S(1)} %get-tuple-element.428), channel_id=1, source_target_pairs={{1,0},{2,1},{3,2},{4,3},{5,4},{6,5},{7,6},{8,7},{9,8},{10,9},{11,1... | collective-permute-start | bytes 786440 | tf_op jit(solution)/shard_map/ppermute | solution.py:14
where the time goes:
time: 104 us
  waiting for transfers between devices  32.2 us (31%)
  starting transfers between devices  31.1 us (30%)
  matrix products  29.1 us (28%)
  other arithmetic  6.8 us (7%)
  local copies, waits for them, and re-layouts  3.08 us (3%)
    ppermute x12, waiting for transfers between devices, shifted(): return lax.ppermute(value, axis, pairs)  32.2 us
    ppermute x12, starting transfers between devices, shifted(): return lax.ppermute(value, axis, pairs)  31.1 us
    dot_general x4, matrix products, sub_block(): jnp.einsum('rd,kd->rk', q_rows, key_rows, preferred_element_type=jnp.floa...  7.18 us
    dot_general x4, matrix products, sub_block(): jnp.einsum('rk,rd->kd', score_grad, q_rows, preferred_element_type=jnp.fl...  5.89 us
    dot_general x4, matrix products, sub_block(): jnp.dot(probs_low, value_rows, preferred_element_type=jnp.float32)  5.09 us
    dot_general x4, matrix products, sub_block(): jnp.dot(score_grad, key_rows, preferred_element_type=jnp.float32)  4.82 us
    dot_general x4, matrix products, sub_block(): jnp.einsum('rd,kd->rk', grad_rows, value_rows, preferred_element_type=jnp...  3.12 us
    dot_general x4, matrix products, sub_block(): jnp.einsum('rk,rd->kd', probs_low, grad_rows, preferred_element_type=jnp....  3.02 us
  transfers between devices with their start and end apart: 12, of which 7 were waited for; matrix products, arithmetic and copies ran while one was open for 1% of the time, Pallas kernels for 0%

commit v1 on v0

v1 whole, which is shorter than its diff:
```python
import functools

import jax
import jax.numpy as jnp
from jax import lax
from jax.experimental import pallas as pl
from jax.experimental.pallas import tpu as pltpu
from jax.sharding import PartitionSpec as P

BLK = 128
WIN = 1024
FAR = 6
ROWS = 256
AXES = ("ctxa", "ctxb")
NEG = -1e30
BIG = 1e30
LOG2E = 1.4426950408889634
NT = (((1,), (1,)), ((), ()))
NN = (((1,), (0,)), ((), ()))


def dot(a, b, dims):
    return lax.dot_general(a, b, dims, preferred_element_type=jnp.float32)


def attention_kernel(plan, *refs):
    tok, heads, width, near, distances = plan
    pieces = len(near) + len(distances)
    q_ref, g_ref = refs[0], refs[1]
    kv_refs = refs[2 : 2 + pieces]
    att_ref, qg_ref = refs[2 + pieces], refs[3 + pieces]
    kvg_refs = refs[4 + pieces : 4 + 2 * pieces]
    k_c, v_c, kt_c, vt_c, dk_c, dv_c, s_c, p_c, d_c, grads = refs[4 + 2 * pieces :]
    per = tok // BLK
    win_blocks = WIN // BLK + 1
    levels = len(distances)
    blocks = win_blocks + levels
    block = pl.program_id(0)
    tile = pl.program_id(1)
    tiles = pl.num_programs(1)
    device = lax.axis_index(AXES)
    scale = 1.0 / width**0.5

    def source(block_index, part):
        if part < win_blocks:
            piece, offset = divmod(block_index + part, per)
            return piece, offset * BLK
        return len(near) + part - win_blocks, block_index * BLK

    def valid(part):
        if part < win_blocks:
            return device * per + block + part >= win_blocks - 1
        return device >= distances[part - win_blocks]

    @pl.when((block == 0) & (tile == 0))
    def _():
        grads[...] = jnp.zeros_like(grads)
        lane = lax.broadcasted_iota(jnp.int32, (blocks * BLK, width), 1)
        v_c[:, width:] = jnp.where(lane < 3, 1.0, 0.0).astype(jnp.bfloat16)
        vt_c[width:, :] = jnp.ones((16, blocks * BLK), jnp.bfloat16)

    for index in range(per):

        @pl.when((block == index) & (tile == 0))
        def _():
            for part in range(blocks):
                piece, offset = source(index, part)
                rows = slice(part * BLK, (part + 1) * BLK)
                keys = kv_refs[piece][0, offset : offset + BLK, :]
                values = kv_refs[piece][1, offset : offset + BLK, :]
                k_c[rows, :width] = keys
                k_c[rows, width:] = keys
                v_c[rows, :width] = values
                kt_c[:, rows] = keys.T
                vt_c[:width, rows] = values.T

    q = q_ref[...]
    g = g_ref[...]
    scaled = q.astype(jnp.float32) * (scale * LOG2E)
    q_hi = scaled.astype(jnp.bfloat16)
    q_lo = (scaled - q_hi.astype(jnp.float32)).astype(jnp.bfloat16)
    q_aug = jnp.concatenate([q_hi, q_lo], axis=1)
    s_c[...] = dot(k_c[...], q_aug, NT)
    key_in = lax.broadcasted_iota(jnp.int32, (BLK, ROWS), 0)
    tok_in = lax.broadcasted_iota(jnp.int32, (BLK, ROWS), 1) // heads + tile * (ROWS // heads)
    newest = slice((win_blocks - 1) * BLK, win_blocks * BLK)
    s_c[:BLK, :] = jnp.where(key_in > tok_in, s_c[:BLK, :], NEG)
    s_c[newest, :] = jnp.where(key_in <= tok_in, s_c[newest, :], NEG)
    top = jnp.full((8, ROWS), NEG, jnp.float32)
    for part in range(blocks):
        rows = slice(part * BLK, (part + 1) * BLK)
        part_top = jnp.max(s_c[rows, :].reshape(BLK // 8, 8, ROWS), axis=0)
        top = jnp.maximum(top, jnp.where(valid(part), part_top, NEG))
    row_max = jnp.max(top, axis=0, keepdims=True)
    for part in range(blocks):
        rows = slice(part * BLK, (part + 1) * BLK)
        shift = jnp.where(valid(part), row_max, BIG)
        p_c[rows, :] = jnp.exp2(s_c[rows, :] - shift).astype(jnp.bfloat16)
    acc = dot(vt_c[...], p_c[...], NN)
    inverse = 1.0 / acc[width : width + 1, :]
    att = (acc[:width, :] * inverse).T.astype(jnp.bfloat16)
    att_ref[...] = att
    g_norm = (g.astype(jnp.float32) * jnp.broadcast_to(inverse, (width, ROWS)).T).astype(jnp.bfloat16)
    delta = -jnp.sum(g_norm.astype(jnp.float32) * att.astype(jnp.float32), axis=1, keepdims=True)
    d_hi = delta.astype(jnp.bfloat16).astype(jnp.float32)
    d_mid = (delta - d_hi).astype(jnp.bfloat16).astype(jnp.float32)
    d_lo = delta - d_hi - d_mid
    lane = lax.broadcasted_iota(jnp.int32, (ROWS, width), 1)
    tail = jnp.where(lane == 0, d_hi, jnp.where(lane == 1, d_mid, jnp.where(lane == 2, d_lo, 0.0)))
    g_aug = jnp.concatenate([g_norm, tail.astype(jnp.bfloat16)], axis=1)
    d_c[...] = (p_c[...].astype(jnp.float32) * dot(v_c[...], g_aug, NT)).astype(jnp.bfloat16)
    dv = dot(p_c[...], g_norm, NN)
    dk = dot(d_c[...], q, NN)

    @pl.when(tile == 0)
    def _():
        dv_c[...] = dv
        dk_c[...] = dk

    @pl.when(tile > 0)
    def _():
        dv_c[...] += dv
        dk_c[...] += dk

    dq = dot(kt_c[...], d_c[...], NN)
    qg_ref[...] = (dq * scale).T.astype(jnp.bfloat16)

    for index in range(per):

        @pl.when((block == index) & (tile == tiles - 1))
        def _():
            for part in range(blocks):
                piece, offset = source(index, part)
                rows = slice(part * BLK, (part + 1) * BLK)
                grads[piece, 0, offset : offset + BLK, :] += dk_c[rows, :] * scale
                grads[piece, 1, offset : offset + BLK, :] += dv_c[rows, :]

    @pl.when((block == per - 1) & (tile == tiles - 1))
    def _():
        for piece in range(pieces):
            kvg_refs[piece][...] = grads[piece].astype(kvg_refs[piece].dtype)


def attend(q_rows, g_rows, kv_pieces, plan):
    tok, heads, width, near, distances = plan
    pieces = len(kv_pieces)
    blocks = WIN // BLK + 1 + len(distances)
    keys = blocks * BLK
    tiles = BLK * heads // ROWS
    row_spec = pl.BlockSpec((ROWS, width), lambda b, t: (b * tiles + t, 0))
    kv_spec = pl.BlockSpec((2, tok, width), lambda b, t: (0, 0, 0))
    row_shape = jax.ShapeDtypeStruct(q_rows.shape, jnp.bfloat16)
    own = len(near) - 1
    kvg_shapes = [
        jax.ShapeDtypeStruct((2, tok, width), jnp.float32 if i == own else jnp.bfloat16)
        for i in range(pieces)
    ]
    bf16, f32 = jnp.bfloat16, jnp.float32
    return pl.pallas_call(
        functools.partial(attention_kernel, plan),
        out_shape=[row_shape, row_shape] + kvg_shapes,
        grid=(tok // BLK, tiles),
        in_specs=[row_spec, row_spec] + [kv_spec] * pieces,
        out_specs=[row_spec, row_spec] + [kv_spec] * pieces,
        scratch_shapes=[
            pltpu.VMEM((keys, 2 * width), bf16),
            pltpu.VMEM((keys, 2 * width), bf16),
            pltpu.VMEM((width, keys), bf16),
            pltpu.VMEM((width + 16, keys), bf16),
            pltpu.VMEM((keys, width), f32),
            pltpu.VMEM((keys, width), f32),
            pltpu.VMEM((keys, ROWS), f32),
            pltpu.VMEM((keys, ROWS), bf16),
            pltpu.VMEM((keys, ROWS), bf16),
            pltpu.VMEM((pieces, 2, tok, width), f32),
        ],
        compiler_params=pltpu.CompilerParams(
            dimension_semantics=("arbitrary", "arbitrary"), vmem_limit_bytes=56 << 20
        ),
    )(q_rows, g_rows, *kv_pieces)


def shifted(value, by):
    count = lax.axis_size(AXES)
    return lax.ppermute(value, AXES, [(i, (i + by) % count) for i in range(count)])


def body(queries, key_vectors, value_vectors, out_grad):
    tok, heads, width = queries.shape
    devices_all = lax.axis_size(AXES)
    device = lax.axis_index(AXES)
    shards = WIN // tok
    stride = 2 * WIN // tok
    paired = jnp.stack([key_vectors, value_vectors])
    distances = tuple(
        stride * 2**level for level in range(FAR) if stride * 2**level < devices_all
    )
    near = tuple(range(shards, -1, -1))
    offsets = near[:-1] + (0,) + distances
    kv_pieces = [paired if by == 0 else shifted(paired, by) for by in offsets]
    plan = (tok, heads, width, near, distances)
    outs = attend(
        queries.reshape(tok * heads, width), out_grad.reshape(tok * heads, width), kv_pieces, plan
    )
    attention, query_grad = outs[0], outs[1]
    own_grad = None
    total = outs[2 + shards]
    for by, terms in zip(offsets, outs[2:]):
        if by:
            total = total + shifted(terms, -by).astype(jnp.float32)
    return (
        attention.reshape(queries.shape),
        query_grad.reshape(queries.shape),
        total[0].astype(jnp.bfloat16),
        total[1].astype(jnp.bfloat16),
    )


def solution(mesh):
    rows = P(AXES, None, None)
    keys = P(AXES, None)
    return jax.shard_map(
        body,
        mesh=mesh,
        in_specs=(rows, keys, keys, rows),
        out_specs=(rows, rows, keys, keys),
        check_vma=False,
    )
```

time: 104 us -> 78.6 us (0.76)
  the two profiles are of different devices: /device:TPU:15 before, /device:TPU:0 now
where the time goes in v1:
time: 78.6 us; the launch traced here: 78.4 us
  starting transfers between devices  26.6 us (34%)
  Pallas kernels  25.7 us (33%)
  waiting for transfers between devices  22.1 us (28%)
  other arithmetic  1.96 us (2%)
  local copies, waits for them, and re-layouts  1.29 us (2%)
    ppermute x12, starting transfers between devices, shifted(): lax.ppermute(value, AXES, [(i, (i + by) % count) for i in range(count)])  26.6 us
    pallas_call x1, Pallas kernels, attend(): pl.pallas_call(functools.partial(attention_kernel, plan), out_shape=[row_...  25.7 us
    ppermute x12, waiting for transfers between devices, shifted(): lax.ppermute(value, AXES, [(i, (i + by) % count) for i in range(count)])  22.1 us
  transfers between devices with their start and end apart: 12, of which 6 were waited for; matrix products, arithmetic and copies ran while one was open for 0% of the time, Pallas kernels for 0%

profile of v1, /device:TPU:0, one launch (start us, length us, event | category | flops | bytes accessed | tf_op | source)
XLA Modules:
  0.0 78.4 jit_solution(12998661844739877582)
XLA Ops:
  0.6 0.9 %pad_maximum_fusion.refs_6_ = bf16[2,256,128]{2,1,0:T(8,128)(2,1)S(1)} fusion(bf16[1,256,128]{2,1,0:T(8,128)(2,1)} %bitcast.12, bf16[1,256,128]{2,1,0:T(8,128)(2,1)} %bitcast.13), kind=kLoop, calls=%fused_computation.1 | loop fusion | flops 65536 | bytes 262144 | tf_op jit(solution)/shard_map/stack | solution.py:194
  1.5 4.1 %collective-permute-start.5 = (bf16[2,256,128]{2,1,0:T(8,128)(2,1)S(1)}, bf16[2,256,128]{2,1,0:T(8,128)(2,1)S(1)}, u32[]{:S(2)}, u32[]{:S(2)}) collective-permute-start(bf16[2,256,128]{2,1,0:T(8,128)(2,1)S(1)} %pad_maximum_fusion.refs_6_), channel_id=1, source_target_pairs={{0,16},{1,17},{2,18},{3,19},{4,20},{5,21},{6,22},{7,23},{8,24},{9,... | collective-permute-start | bytes 393224 | tf_op jit(solution)/shard_map/ppermute | solution.py:185
  5.7 1.6 %collective-permute-start.4 = (bf16[2,256,128]{2,1,0:T(8,128)(2,1)S(1)}, bf16[2,256,128]{2,1,0:T(8,128)(2,1)S(1)}, u32[]{:S(2)}, u32[]{:S(2)}) collective-permute-start(bf16[2,256,128]{2,1,0:T(8,128)(2,1)S(1)} %pad_maximum_fusion.refs_6_), channel_id=1, source_target_pairs={{0,8},{1,9},{2,10},{3,11},{4,12},{5,13},{6,14},{7,15},{8,16},{9,17... | collective-permute-start | bytes 393224 | tf_op jit(solution)/shard_map/ppermute | solution.py:185
  7.2 0.0 collective-permute-start.3
  7.2 1.5 %collective-permute-start.2 = (bf16[2,256,128]{2,1,0:T(8,128)(2,1)S(1)}, bf16[2,256,128]{2,1,0:T(8,128)(2,1)S(1)}, u32[]{:S(2)}, u32[]{:S(2)}) collective-permute-start(bf16[2,256,128]{2,1,0:T(8,128)(2,1)S(1)} %pad_maximum_fusion.refs_6_), channel_id=1, source_target_pairs={{0,2},{1,3},{2,4},{3,5},{4,6},{5,7},{6,8},{7,9},{8,10},{9,11},{10,... | collective-permute-start | bytes 393224 | tf_op jit(solution)/shard_map/ppermute | solution.py:185
  8.7 2.4 %collective-permute-start.1 = (bf16[2,256,128]{2,1,0:T(8,128)(2,1)S(1)}, bf16[2,256,128]{2,1,0:T(8,128)(2,1)S(1)}, u32[]{:S(2)}, u32[]{:S(2)}) collective-permute-start(bf16[2,256,128]{2,1,0:T(8,128)(2,1)S(1)} %pad_maximum_fusion.refs_6_), channel_id=1, source_target_pairs={{0,3},{1,4},{2,5},{3,6},{4,7},{5,8},{6,9},{7,10},{8,11},{9,12},{10... | collective-permute-start | bytes 393224 | tf_op jit(solution)/shard_map/ppermute | solution.py:185
  11.2 3.6 %collective-permute-done.5.refs_8_ = bf16[2,256,128]{2,1,0:T(8,128)(2,1)S(1)} collective-permute-done((bf16[2,256,128]{2,1,0:T(8,128)(2,1)S(1)}, bf16[2,256,128]{2,1,0:T(8,128)(2,1)S(1)}, u32[]{:S(2)}, u32[]{:S(2)}) %collective-permute-start.5) | collective-permute-done | bytes 131104 | tf_op jit(solution)/shard_map/ppermute | solution.py:185
  14.8 3.2 %collective-permute-start = (bf16[2,256,128]{2,1,0:T(8,128)(2,1)S(1)}, bf16[2,256,128]{2,1,0:T(8,128)(2,1)S(1)}, u32[]{:S(2)}, u32[]{:S(2)}) collective-permute-start(bf16[2,256,128]{2,1,0:T(8,128)(2,1)S(1)} %pad_maximum_fusion.refs_6_), channel_id=1, source_target_pairs={{0,4},{1,5},{2,6},{3,7},{4,8},{5,9},{6,10},{7,11},{8,12},{9,13},{1... | collective-permute-start | bytes 393224 | tf_op jit(solution)/shard_map/ppermute | solution.py:185
  17.9 0.0 collective-permute-done.4.refs_7_
  17.9 0.0 collective-permute-done.3.refs_5_
  18.0 1.3 %collective-permute-done.2.refs_4_ = bf16[2,256,128]{2,1,0:T(8,128)(2,1)S(1)} collective-permute-done((bf16[2,256,128]{2,1,0:T(8,128)(2,1)S(1)}, bf16[2,256,128]{2,1,0:T(8,128)(2,1)S(1)}, u32[]{:S(2)}, u32[]{:S(2)}) %collective-permute-start.2) | collective-permute-done | bytes 131104 | tf_op jit(solution)/shard_map/ppermute | solution.py:185
  19.3 4.9 %collective-permute-done.refs_2_ = bf16[2,256,128]{2,1,0:T(8,128)(2,1)S(1)} collective-permute-done((bf16[2,256,128]{2,1,0:T(8,128)(2,1)S(1)}, bf16[2,256,128]{2,1,0:T(8,128)(2,1)S(1)}, u32[]{:S(2)}, u32[]{:S(2)}) %collective-permute-start) | collective-permute-done | bytes 131104 | tf_op jit(solution)/shard_map/ppermute | solution.py:185
  24.2 0.6 copy-done.6
  24.8 25.7 %shard_map.75 = (bf16[2048,128]{1,0:T(8,128)(2,1)}, bf16[2048,128]{1,0:T(8,128)(2,1)}, bf16[2,256,128]{2,1,0:T(8,128)(2,1)}, bf16[2,256,128]{2,1,0:T(8,128)(2,1)...) custom-call(bf16[2048,128]{1,0:T(8,128)(2,1)} %bitcast.10, ...), custom_call_target="tpu_custom_call" | custom-call | tf_op jit(solution)/shard_map/pallas_call | solution.py:159
  50.5 0.1 collective-permute-start.6
  50.6 1.9 %collective-permute-start.7 = (bf16[2,256,128]{2,1,0:T(8,128)(2,1)}, bf16[2,256,128]{2,1,0:T(8,128)(2,1)S(1)}, u32[]{:S(2)}, u32[]{:S(2)}) collective-permute-start(bf16[2,256,128]{2,1,0:T(8,128)(2,1)} %get-tuple-element.17), channel_id=1, source_target_pairs={{0,29},{1,30},{2,31},{3,0},{4,1},{5,2},{6,3},{7,4},{8,5},{9,6},{10... | collective-permute-start | bytes 393224 | tf_op jit(solution)/shard_map/ppermute | solution.py:185
  52.5 6.4 %collective-permute-start.8 = (bf16[2,256,128]{2,1,0:T(8,128)(2,1)}, bf16[2,256,128]{2,1,0:T(8,128)(2,1)S(1)}, u32[]{:S(2)}, u32[]{:S(2)}) collective-permute-start(bf16[2,256,128]{2,1,0:T(8,128)(2,1)} %get-tuple-element.18), channel_id=1, source_target_pairs={{0,30},{1,31},{2,0},{3,1},{4,2},{5,3},{6,4},{7,5},{8,6},{9,7},{10,... | collective-permute-start | bytes 393224 | tf_op jit(solution)/shard_map/ppermute | solution.py:185
  58.9 2.9 %collective-permute-start.9 = (bf16[2,256,128]{2,1,0:T(8,128)(2,1)}, bf16[2,256,128]{2,1,0:T(8,128)(2,1)S(1)}, u32[]{:S(2)}, u32[]{:S(2)}) collective-permute-start(bf16[2,256,128]{2,1,0:T(8,128)(2,1)} %get-tuple-element.19), channel_id=1, source_target_pairs={{0,31},{1,0},{2,1},{3,2},{4,3},{5,4},{6,5},{7,6},{8,7},{9,8},{10,9... | collective-permute-start | bytes 393224 | tf_op jit(solution)/shard_map/ppermute | solution.py:185
  61.8 2.5 %collective-permute-start.11 = (bf16[2,256,128]{2,1,0:T(8,128)(2,1)}, bf16[2,256,128]{2,1,0:T(8,128)(2,1)S(1)}, u32[]{:S(2)}, u32[]{:S(2)}) collective-permute-start(bf16[2,256,128]{2,1,0:T(8,128)(2,1)} %get-tuple-element.21), channel_id=1, source_target_pairs={{0,16},{1,17},{2,18},{3,19},{4,20},{5,21},{6,22},{7,23},{8,24},{9,... | collective-permute-start | bytes 393224 | tf_op jit(solution)/shard_map/ppermute | solution.py:185
  64.4 1.7 %collective-permute-done.9 = bf16[2,256,128]{2,1,0:T(8,128)(2,1)S(1)} collective-permute-done((bf16[2,256,128]{2,1,0:T(8,128)(2,1)}, bf16[2,256,128]{2,1,0:T(8,128)(2,1)S(1)}, u32[]{:S(2)}, u32[]{:S(2)}) %collective-permute-start.9) | collective-permute-done | bytes 131104 | tf_op jit(solution)/shard_map/ppermute | solution.py:185
  66.1 6.8 %collective-permute-done.10 = bf16[2,256,128]{2,1,0:T(8,128)(2,1)S(1)} collective-permute-done((bf16[2,256,128]{2,1,0:T(8,128)(2,1)}, bf16[2,256,128]{2,1,0:T(8,128)(2,1)S(1)}, u32[]{:S(2)}, u32[]{:S(2)}) %collective-permute-start.10) | collective-permute-done | bytes 131104 | tf_op jit(solution)/shard_map/ppermute | solution.py:185
  72.9 3.8 %collective-permute-done.11 = bf16[2,256,128]{2,1,0:T(8,128)(2,1)S(1)} collective-permute-done((bf16[2,256,128]{2,1,0:T(8,128)(2,1)}, bf16[2,256,128]{2,1,0:T(8,128)(2,1)S(1)}, u32[]{:S(2)}, u32[]{:S(2)}) %collective-permute-start.11) | collective-permute-done | bytes 131104 | tf_op jit(solution)/shard_map/ppermute | solution.py:185
  76.7 1.1 %add_convert_fusion = bf16[2,256,128]{2,1,0:T(8,128)(2,1)S(1)} fusion(bf16[2,256,128]{2,1,0:T(8,128)(2,1)S(1)} %collective-permute-done.11, bf16[2,256,128]{2,1,0:T(8,128)(2,1)S(1)} %collective-permute-done.10, bf16[2,256,128]{2,1,0:T(8,128)(2,1)S(1)} %collective-permute-done.9, bf16[2,256,128]{2,1,0:T(8,128)(2,1)S(1)} %collective-permute-done.8, ...), kind=kLoop, calls=%fused_computation | loop fusion | flops 851968 | bytes 1179648 | tf_op jit(solution)/shard_map/convert.1
  77.7 0.7 slice_bitcast_fusion
  (18 shorter events, 0.0 us)
Async XLA Ops:
  1.5 22.7 %copy-start = (bf16[2,256,128]{2,1,0:T(8,128)(2,1)}, bf16[2,256,128]{2,1,0:T(8,128)(2,1)S(1)}, u32[]{:S(2)}) copy-start(bf16[2,256,128]{2,1,0:T(8,128)(2,1)S(1)} %pad_maximum_fusion.refs_6_) | copy-start | bytes 393220
  1.5 13.2 %collective-permute-start.5 = (bf16[2,256,128]{2,1,0:T(8,128)(2,1)S(1)}, bf16[2,256,128]{2,1,0:T(8,128)(2,1)S(1)}, u32[]{:S(2)}, u32[]{:S(2)}) collective-permute-start(bf16[2,256,128]{2,1,0:T(8,128)(2,1)S(1)} %pad_maximum_fusion.refs_6_), channel_id=1, source_target_pairs={{0,16},{1,17},{2,18},{3,19},{4,20},{5,21},{6,22},{7,23},{8,24},{9,... | collective-permute-start | bytes 393224 | tf_op jit(solution)/shard_map/ppermute | solution.py:185
  5.7 12.3 %collective-permute-start.4 = (bf16[2,256,128]{2,1,0:T(8,128)(2,1)S(1)}, bf16[2,256,128]{2,1,0:T(8,128)(2,1)S(1)}, u32[]{:S(2)}, u32[]{:S(2)}) collective-permute-start(bf16[2,256,128]{2,1,0:T(8,128)(2,1)S(1)} %pad_maximum_fusion.refs_6_), channel_id=1, source_target_pairs={{0,8},{1,9},{2,10},{3,11},{4,12},{5,13},{6,14},{7,15},{8,16},{9,17... | collective-permute-start | bytes 393224 | tf_op jit(solution)/shard_map/ppermute | solution.py:185
  7.2 10.7 %collective-permute-start.3 = (bf16[2,256,128]{2,1,0:T(8,128)(2,1)S(1)}, bf16[2,256,128]{2,1,0:T(8,128)(2,1)S(1)}, u32[]{:S(2)}, u32[]{:S(2)}) collective-permute-start(bf16[2,256,128]{2,1,0:T(8,128)(2,1)S(1)} %pad_maximum_fusion.refs_6_), channel_id=1, source_target_pairs={{0,1},{1,2},{2,3},{3,4},{4,5},{5,6},{6,7},{7,8},{8,9},{9,10},{10,1... | collective-permute-start | bytes 393224 | tf_op jit(solution)/shard_map/ppermute | solution.py:185
  7.2 12.1 %collective-permute-start.2 = (bf16[2,256,128]{2,1,0:T(8,128)(2,1)S(1)}, bf16[2,256,128]{2,1,0:T(8,128)(2,1)S(1)}, u32[]{:S(2)}, u32[]{:S(2)}) collective-permute-start(bf16[2,256,128]{2,1,0:T(8,128)(2,1)S(1)} %pad_maximum_fusion.refs_6_), channel_id=1, source_target_pairs={{0,2},{1,3},{2,4},{3,5},{4,6},{5,7},{6,8},{7,9},{8,10},{9,11},{10,... | collective-permute-start | bytes 393224 | tf_op jit(solution)/shard_map/ppermute | solution.py:185
  8.7 10.6 %collective-permute-start.1 = (bf16[2,256,128]{2,1,0:T(8,128)(2,1)S(1)}, bf16[2,256,128]{2,1,0:T(8,128)(2,1)S(1)}, u32[]{:S(2)}, u32[]{:S(2)}) collective-permute-start(bf16[2,256,128]{2,1,0:T(8,128)(2,1)S(1)} %pad_maximum_fusion.refs_6_), channel_id=1, source_target_pairs={{0,3},{1,4},{2,5},{3,6},{4,7},{5,8},{6,9},{7,10},{8,11},{9,12},{10... | collective-permute-start | bytes 393224 | tf_op jit(solution)/shard_map/ppermute | solution.py:185
  14.8 9.4 %copy-start.1 = (bf16[2,256,128]{2,1,0:T(8,128)(2,1)}, bf16[2,256,128]{2,1,0:T(8,128)(2,1)S(1)}, u32[]{:S(2)}) copy-start(bf16[2,256,128]{2,1,0:T(8,128)(2,1)S(1)} %collective-permute-done.5.refs_8_) | copy-start | bytes 393220
  14.8 9.4 %collective-permute-start = (bf16[2,256,128]{2,1,0:T(8,128)(2,1)S(1)}, bf16[2,256,128]{2,1,0:T(8,128)(2,1)S(1)}, u32[]{:S(2)}, u32[]{:S(2)}) collective-permute-start(bf16[2,256,128]{2,1,0:T(8,128)(2,1)S(1)} %pad_maximum_fusion.refs_6_), channel_id=1, source_target_pairs={{0,4},{1,5},{2,6},{3,7},{4,8},{5,9},{6,10},{7,11},{8,12},{9,13},{1... | collective-permute-start | bytes 393224 | tf_op jit(solution)/shard_map/ppermute | solution.py:185
  17.9 6.2 %copy-start.2 = (bf16[2,256,128]{2,1,0:T(8,128)(2,1)}, bf16[2,256,128]{2,1,0:T(8,128)(2,1)S(1)}, u32[]{:S(2)}) copy-start(bf16[2,256,128]{2,1,0:T(8,128)(2,1)S(1)} %collective-permute-done.4.refs_7_) | copy-start | bytes 393220
  17.9 6.2 %copy-start.3 = (bf16[2,256,128]{2,1,0:T(8,128)(2,1)}, bf16[2,256,128]{2,1,0:T(8,128)(2,1)S(1)}, u32[]{:S(2)}) copy-start(bf16[2,256,128]{2,1,0:T(8,128)(2,1)S(1)} %collective-permute-done.3.refs_5_) | copy-start | bytes 393220
  19.3 4.9 %copy-start.4 = (bf16[2,256,128]{2,1,0:T(8,128)(2,1)}, bf16[2,256,128]{2,1,0:T(8,128)(2,1)S(1)}, u32[]{:S(2)}) copy-start(bf16[2,256,128]{2,1,0:T(8,128)(2,1)S(1)} %collective-permute-done.2.refs_4_) | copy-start | bytes 393220
  19.3 4.9 %copy-start.5 = (bf16[2,256,128]{2,1,0:T(8,128)(2,1)}, bf16[2,256,128]{2,1,0:T(8,128)(2,1)S(1)}, u32[]{:S(2)}) copy-start(bf16[2,256,128]{2,1,0:T(8,128)(2,1)S(1)} %collective-permute-done.1.refs_3_) | copy-start | bytes 393220
  24.2 0.6 copy-start.6
  50.5 11.3 %collective-permute-start.6 = (bf16[2,256,128]{2,1,0:T(8,128)(2,1)}, bf16[2,256,128]{2,1,0:T(8,128)(2,1)S(1)}, u32[]{:S(2)}, u32[]{:S(2)}) collective-permute-start(bf16[2,256,128]{2,1,0:T(8,128)(2,1)} %get-tuple-element.16), channel_id=1, source_target_pairs={{0,28},{1,29},{2,30},{3,31},{4,0},{5,1},{6,2},{7,3},{8,4},{9,5},{1... | collective-permute-start | bytes 393224 | tf_op jit(solution)/shard_map/ppermute | solution.py:185
  50.6 13.8 %collective-permute-start.7 = (bf16[2,256,128]{2,1,0:T(8,128)(2,1)}, bf16[2,256,128]{2,1,0:T(8,128)(2,1)S(1)}, u32[]{:S(2)}, u32[]{:S(2)}) collective-permute-start(bf16[2,256,128]{2,1,0:T(8,128)(2,1)} %get-tuple-element.17), channel_id=1, source_target_pairs={{0,29},{1,30},{2,31},{3,0},{4,1},{5,2},{6,3},{7,4},{8,5},{9,6},{10... | collective-permute-start | bytes 393224 | tf_op jit(solution)/shard_map/ppermute | solution.py:185
  52.5 11.9 %collective-permute-start.8 = (bf16[2,256,128]{2,1,0:T(8,128)(2,1)}, bf16[2,256,128]{2,1,0:T(8,128)(2,1)S(1)}, u32[]{:S(2)}, u32[]{:S(2)}) collective-permute-start(bf16[2,256,128]{2,1,0:T(8,128)(2,1)} %get-tuple-element.18), channel_id=1, source_target_pairs={{0,30},{1,31},{2,0},{3,1},{4,2},{5,3},{6,4},{7,5},{8,6},{9,7},{10,... | collective-permute-start | bytes 393224 | tf_op jit(solution)/shard_map/ppermute | solution.py:185
  58.9 7.2 %collective-permute-start.9 = (bf16[2,256,128]{2,1,0:T(8,128)(2,1)}, bf16[2,256,128]{2,1,0:T(8,128)(2,1)S(1)}, u32[]{:S(2)}, u32[]{:S(2)}) collective-permute-start(bf16[2,256,128]{2,1,0:T(8,128)(2,1)} %get-tuple-element.19), channel_id=1, source_target_pairs={{0,31},{1,0},{2,1},{3,2},{4,3},{5,4},{6,5},{7,6},{8,7},{9,8},{10,9... | collective-permute-start | bytes 393224 | tf_op jit(solution)/shard_map/ppermute | solution.py:185
  61.8 11.1 %collective-permute-start.10 = (bf16[2,256,128]{2,1,0:T(8,128)(2,1)}, bf16[2,256,128]{2,1,0:T(8,128)(2,1)S(1)}, u32[]{:S(2)}, u32[]{:S(2)}) collective-permute-start(bf16[2,256,128]{2,1,0:T(8,128)(2,1)} %get-tuple-element.20), channel_id=1, source_target_pairs={{0,24},{1,25},{2,26},{3,27},{4,28},{5,29},{6,30},{7,31},{8,0},{9,1... | collective-permute-start | bytes 393224 | tf_op jit(solution)/shard_map/ppermute | solution.py:185
  61.8 14.8 %collective-permute-start.11 = (bf16[2,256,128]{2,1,0:T(8,128)(2,1)}, bf16[2,256,128]{2,1,0:T(8,128)(2,1)S(1)}, u32[]{:S(2)}, u32[]{:S(2)}) collective-permute-start(bf16[2,256,128]{2,1,0:T(8,128)(2,1)} %get-tuple-element.21), channel_id=1, source_target_pairs={{0,16},{1,17},{2,18},{3,19},{4,20},{5,21},{6,22},{7,23},{8,24},{9,... | collective-permute-start | bytes 393224 | tf_op jit(solution)/shard_map/ppermute | solution.py:185

commit v2 on v1

--- a/solution.py
+++ b/solution.py
@@ -10,7 +10,7 @@
 BLK = 128
 WIN = 1024
 FAR = 6
-ROWS = 256
+ROWS = 1024
 AXES = ("ctxa", "ctxb")
 NEG = -1e30
 BIG = 1e30

time: 78.6 us -> 66.2 us (0.84)
  Pallas kernels: 25.7 us -> 13.3 us
    pallas_call x1, Pallas kernels: 25.7 us -> 13.3 us  [attend(): pl.pallas_call(functools.partial(attention_kernel, plan), out_shape=[row_...]
where the time goes in v2:
time: 66.2 us; the launch traced here: 66 us
  starting transfers between devices  26.6 us (40%)
  waiting for transfers between devices  22.1 us (33%)
  Pallas kernels  13.3 us (20%)
  other arithmetic  1.96 us (3%)
  local copies, waits for them, and re-layouts  1.29 us (2%)
  between operations  0.71 us (1%)
    ppermute x12, starting transfers between devices, shifted(): lax.ppermute(value, AXES, [(i, (i + by) % count) for i in range(count)])  26.6 us
    ppermute x12, waiting for transfers between devices, shifted(): lax.ppermute(value, AXES, [(i, (i + by) % count) for i in range(count)])  22.1 us
    pallas_call x1, Pallas kernels, attend(): pl.pallas_call(functools.partial(attention_kernel, plan), out_shape=[row_...  13.3 us
  transfers between devices with their start and end apart: 12, of which 6 were waited for; matrix products, arithmetic and copies ran while one was open for 0% of the time, Pallas kernels for 0%

profile of v2, /device:TPU:0, one launch (start us, length us, event | category | flops | bytes accessed | tf_op | source)
XLA Modules:
  0.0 66.0 jit_solution(15216677958771340578)
XLA Ops:
  0.6 0.9 %pad_maximum_fusion.refs_6_ = bf16[2,256,128]{2,1,0:T(8,128)(2,1)S(1)} fusion(bf16[1,256,128]{2,1,0:T(8,128)(2,1)} %bitcast.12, bf16[1,256,128]{2,1,0:T(8,128)(2,1)} %bitcast.13), kind=kLoop, calls=%fused_computation.1 | loop fusion | flops 65536 | bytes 262144 | tf_op jit(solution)/shard_map/stack | solution.py:194
  1.5 4.1 %collective-permute-start.5 = (bf16[2,256,128]{2,1,0:T(8,128)(2,1)S(1)}, bf16[2,256,128]{2,1,0:T(8,128)(2,1)S(1)}, u32[]{:S(2)}, u32[]{:S(2)}) collective-permute-start(bf16[2,256,128]{2,1,0:T(8,128)(2,1)S(1)} %pad_maximum_fusion.refs_6_), channel_id=1, source_target_pairs={{0,16},{1,17},{2,18},{3,19},{4,20},{5,21},{6,22},{7,23},{8,24},{9,... | collective-permute-start | bytes 393224 | tf_op jit(solution)/shard_map/ppermute | solution.py:185
  5.7 1.6 %collective-permute-start.4 = (bf16[2,256,128]{2,1,0:T(8,128)(2,1)S(1)}, bf16[2,256,128]{2,1,0:T(8,128)(2,1)S(1)}, u32[]{:S(2)}, u32[]{:S(2)}) collective-permute-start(bf16[2,256,128]{2,1,0:T(8,128)(2,1)S(1)} %pad_maximum_fusion.refs_6_), channel_id=1, source_target_pairs={{0,8},{1,9},{2,10},{3,11},{4,12},{5,13},{6,14},{7,15},{8,16},{9,17... | collective-permute-start | bytes 393224 | tf_op jit(solution)/shard_map/ppermute | solution.py:185
  7.2 0.0 collective-permute-start.3
  7.2 1.5 %collective-permute-start.2 = (bf16[2,256,128]{2,1,0:T(8,128)(2,1)S(1)}, bf16[2,256,128]{2,1,0:T(8,128)(2,1)S(1)}, u32[]{:S(2)}, u32[]{:S(2)}) collective-permute-start(bf16[2,256,128]{2,1,0:T(8,128)(2,1)S(1)} %pad_maximum_fusion.refs_6_), channel_id=1, source_target_pairs={{0,2},{1,3},{2,4},{3,5},{4,6},{5,7},{6,8},{7,9},{8,10},{9,11},{10,... | collective-permute-start | bytes 393224 | tf_op jit(solution)/shard_map/ppermute | solution.py:185
  8.7 2.4 %collective-permute-start.1 = (bf16[2,256,128]{2,1,0:T(8,128)(2,1)S(1)}, bf16[2,256,128]{2,1,0:T(8,128)(2,1)S(1)}, u32[]{:S(2)}, u32[]{:S(2)}) collective-permute-start(bf16[2,256,128]{2,1,0:T(8,128)(2,1)S(1)} %pad_maximum_fusion.refs_6_), channel_id=1, source_target_pairs={{0,3},{1,4},{2,5},{3,6},{4,7},{5,8},{6,9},{7,10},{8,11},{9,12},{10... | collective-permute-start | bytes 393224 | tf_op jit(solution)/shard_map/ppermute | solution.py:185
  11.2 3.6 %collective-permute-done.5.refs_8_ = bf16[2,256,128]{2,1,0:T(8,128)(2,1)S(1)} collective-permute-done((bf16[2,256,128]{2,1,0:T(8,128)(2,1)S(1)}, bf16[2,256,128]{2,1,0:T(8,128)(2,1)S(1)}, u32[]{:S(2)}, u32[]{:S(2)}) %collective-permute-start.5) | collective-permute-done | bytes 131104 | tf_op jit(solution)/shard_map/ppermute | solution.py:185
  14.8 3.2 %collective-permute-start = (bf16[2,256,128]{2,1,0:T(8,128)(2,1)S(1)}, bf16[2,256,128]{2,1,0:T(8,128)(2,1)S(1)}, u32[]{:S(2)}, u32[]{:S(2)}) collective-permute-start(bf16[2,256,128]{2,1,0:T(8,128)(2,1)S(1)} %pad_maximum_fusion.refs_6_), channel_id=1, source_target_pairs={{0,4},{1,5},{2,6},{3,7},{4,8},{5,9},{6,10},{7,11},{8,12},{9,13},{1... | collective-permute-start | bytes 393224 | tf_op jit(solution)/shard_map/ppermute | solution.py:185
  17.9 0.0 collective-permute-done.4.refs_7_
  17.9 0.0 collective-permute-done.3.refs_5_
  18.0 1.3 %collective-permute-done.2.refs_4_ = bf16[2,256,128]{2,1,0:T(8,128)(2,1)S(1)} collective-permute-done((bf16[2,256,128]{2,1,0:T(8,128)(2,1)S(1)}, bf16[2,256,128]{2,1,0:T(8,128)(2,1)S(1)}, u32[]{:S(2)}, u32[]{:S(2)}) %collective-permute-start.2) | collective-permute-done | bytes 131104 | tf_op jit(solution)/shard_map/ppermute | solution.py:185
  19.3 4.9 %collective-permute-done.refs_2_ = bf16[2,256,128]{2,1,0:T(8,128)(2,1)S(1)} collective-permute-done((bf16[2,256,128]{2,1,0:T(8,128)(2,1)S(1)}, bf16[2,256,128]{2,1,0:T(8,128)(2,1)S(1)}, u32[]{:S(2)}, u32[]{:S(2)}) %collective-permute-start) | collective-permute-done | bytes 131104 | tf_op jit(solution)/shard_map/ppermute | solution.py:185
  24.2 0.6 copy-done.6
  24.8 13.3 %shard_map.75 = (bf16[2048,128]{1,0:T(8,128)(2,1)}, bf16[2048,128]{1,0:T(8,128)(2,1)}, bf16[2,256,128]{2,1,0:T(8,128)(2,1)}, bf16[2,256,128]{2,1,0:T(8,128)(2,1)...) custom-call(bf16[2048,128]{1,0:T(8,128)(2,1)} %bitcast.10, ...), custom_call_target="tpu_custom_call" | custom-call | tf_op jit(solution)/shard_map/pallas_call | solution.py:159
  38.1 0.1 collective-permute-start.6
  38.2 2.0 %collective-permute-start.7 = (bf16[2,256,128]{2,1,0:T(8,128)(2,1)}, bf16[2,256,128]{2,1,0:T(8,128)(2,1)S(1)}, u32[]{:S(2)}, u32[]{:S(2)}) collective-permute-start(bf16[2,256,128]{2,1,0:T(8,128)(2,1)} %get-tuple-element.17), channel_id=1, source_target_pairs={{0,29},{1,30},{2,31},{3,0},{4,1},{5,2},{6,3},{7,4},{8,5},{9,6},{10... | collective-permute-start | bytes 393224 | tf_op jit(solution)/shard_map/ppermute | solution.py:185
  40.1 6.4 %collective-permute-start.8 = (bf16[2,256,128]{2,1,0:T(8,128)(2,1)}, bf16[2,256,128]{2,1,0:T(8,128)(2,1)S(1)}, u32[]{:S(2)}, u32[]{:S(2)}) collective-permute-start(bf16[2,256,128]{2,1,0:T(8,128)(2,1)} %get-tuple-element.18), channel_id=1, source_target_pairs={{0,30},{1,31},{2,0},{3,1},{4,2},{5,3},{6,4},{7,5},{8,6},{9,7},{10,... | collective-permute-start | bytes 393224 | tf_op jit(solution)/shard_map/ppermute | solution.py:185
  46.5 2.9 %collective-permute-start.9 = (bf16[2,256,128]{2,1,0:T(8,128)(2,1)}, bf16[2,256,128]{2,1,0:T(8,128)(2,1)S(1)}, u32[]{:S(2)}, u32[]{:S(2)}) collective-permute-start(bf16[2,256,128]{2,1,0:T(8,128)(2,1)} %get-tuple-element.19), channel_id=1, source_target_pairs={{0,31},{1,0},{2,1},{3,2},{4,3},{5,4},{6,5},{7,6},{8,7},{9,8},{10,9... | collective-permute-start | bytes 393224 | tf_op jit(solution)/shard_map/ppermute | solution.py:185
  49.5 2.5 %collective-permute-start.11 = (bf16[2,256,128]{2,1,0:T(8,128)(2,1)}, bf16[2,256,128]{2,1,0:T(8,128)(2,1)S(1)}, u32[]{:S(2)}, u32[]{:S(2)}) collective-permute-start(bf16[2,256,128]{2,1,0:T(8,128)(2,1)} %get-tuple-element.21), channel_id=1, source_target_pairs={{0,16},{1,17},{2,18},{3,19},{4,20},{5,21},{6,22},{7,23},{8,24},{9,... | collective-permute-start | bytes 393224 | tf_op jit(solution)/shard_map/ppermute | solution.py:185
  52.0 1.7 %collective-permute-done.9 = bf16[2,256,128]{2,1,0:T(8,128)(2,1)S(1)} collective-permute-done((bf16[2,256,128]{2,1,0:T(8,128)(2,1)}, bf16[2,256,128]{2,1,0:T(8,128)(2,1)S(1)}, u32[]{:S(2)}, u32[]{:S(2)}) %collective-permute-start.9) | collective-permute-done | bytes 131104 | tf_op jit(solution)/shard_map/ppermute | solution.py:185
  53.7 6.8 %collective-permute-done.10 = bf16[2,256,128]{2,1,0:T(8,128)(2,1)S(1)} collective-permute-done((bf16[2,256,128]{2,1,0:T(8,128)(2,1)}, bf16[2,256,128]{2,1,0:T(8,128)(2,1)S(1)}, u32[]{:S(2)}, u32[]{:S(2)}) %collective-permute-start.10) | collective-permute-done | bytes 131104 | tf_op jit(solution)/shard_map/ppermute | solution.py:185
  60.5 3.8 %collective-permute-done.11 = bf16[2,256,128]{2,1,0:T(8,128)(2,1)S(1)} collective-permute-done((bf16[2,256,128]{2,1,0:T(8,128)(2,1)}, bf16[2,256,128]{2,1,0:T(8,128)(2,1)S(1)}, u32[]{:S(2)}, u32[]{:S(2)}) %collective-permute-start.11) | collective-permute-done | bytes 131104 | tf_op jit(solution)/shard_map/ppermute | solution.py:185
  64.3 1.1 %add_convert_fusion = bf16[2,256,128]{2,1,0:T(8,128)(2,1)S(1)} fusion(bf16[2,256,128]{2,1,0:T(8,128)(2,1)S(1)} %collective-permute-done.11, bf16[2,256,128]{2,1,0:T(8,128)(2,1)S(1)} %collective-permute-done.10, bf16[2,256,128]{2,1,0:T(8,128)(2,1)S(1)} %collective-permute-done.9, bf16[2,256,128]{2,1,0:T(8,128)(2,1)S(1)} %collective-permute-done.8, ...), kind=kLoop, calls=%fused_computation | loop fusion | flops 851968 | bytes 1179648 | tf_op jit(solution)/shard_map/convert.1
  65.4 0.7 %slice_bitcast_fusion = (bf16[256,128]{1,0:T(8,128)(2,1)}, bf16[256,128]{1,0:T(8,128)(2,1)}) fusion(bf16[2,256,128]{2,1,0:T(8,128)(2,1)S(1)} %add_convert_fusion), kind=kLoop, calls=%fused_computation.2 | loop fusion | bytes 262144 | tf_op jit(solution)/shard_map/convert_element_type | solution.py:215
  (18 shorter events, 0.0 us)
Async XLA Ops:
  1.5 22.7 %copy-start = (bf16[2,256,128]{2,1,0:T(8,128)(2,1)}, bf16[2,256,128]{2,1,0:T(8,128)(2,1)S(1)}, u32[]{:S(2)}) copy-start(bf16[2,256,128]{2,1,0:T(8,128)(2,1)S(1)} %pad_maximum_fusion.refs_6_) | copy-start | bytes 393220
  1.5 13.2 %collective-permute-start.5 = (bf16[2,256,128]{2,1,0:T(8,128)(2,1)S(1)}, bf16[2,256,128]{2,1,0:T(8,128)(2,1)S(1)}, u32[]{:S(2)}, u32[]{:S(2)}) collective-permute-start(bf16[2,256,128]{2,1,0:T(8,128)(2,1)S(1)} %pad_maximum_fusion.refs_6_), channel_id=1, source_target_pairs={{0,16},{1,17},{2,18},{3,19},{4,20},{5,21},{6,22},{7,23},{8,24},{9,... | collective-permute-start | bytes 393224 | tf_op jit(solution)/shard_map/ppermute | solution.py:185
  5.7 12.3 %collective-permute-start.4 = (bf16[2,256,128]{2,1,0:T(8,128)(2,1)S(1)}, bf16[2,256,128]{2,1,0:T(8,128)(2,1)S(1)}, u32[]{:S(2)}, u32[]{:S(2)}) collective-permute-start(bf16[2,256,128]{2,1,0:T(8,128)(2,1)S(1)} %pad_maximum_fusion.refs_6_), channel_id=1, source_target_pairs={{0,8},{1,9},{2,10},{3,11},{4,12},{5,13},{6,14},{7,15},{8,16},{9,17... | collective-permute-start | bytes 393224 | tf_op jit(solution)/shard_map/ppermute | solution.py:185
  7.2 10.7 %collective-permute-start.3 = (bf16[2,256,128]{2,1,0:T(8,128)(2,1)S(1)}, bf16[2,256,128]{2,1,0:T(8,128)(2,1)S(1)}, u32[]{:S(2)}, u32[]{:S(2)}) collective-permute-start(bf16[2,256,128]{2,1,0:T(8,128)(2,1)S(1)} %pad_maximum_fusion.refs_6_), channel_id=1, source_target_pairs={{0,1},{1,2},{2,3},{3,4},{4,5},{5,6},{6,7},{7,8},{8,9},{9,10},{10,1... | collective-permute-start | bytes 393224 | tf_op jit(solution)/shard_map/ppermute | solution.py:185
  7.2 12.1 %collective-permute-start.2 = (bf16[2,256,128]{2,1,0:T(8,128)(2,1)S(1)}, bf16[2,256,128]{2,1,0:T(8,128)(2,1)S(1)}, u32[]{:S(2)}, u32[]{:S(2)}) collective-permute-start(bf16[2,256,128]{2,1,0:T(8,128)(2,1)S(1)} %pad_maximum_fusion.refs_6_), channel_id=1, source_target_pairs={{0,2},{1,3},{2,4},{3,5},{4,6},{5,7},{6,8},{7,9},{8,10},{9,11},{10,... | collective-permute-start | bytes 393224 | tf_op jit(solution)/shard_map/ppermute | solution.py:185
  8.7 10.6 %collective-permute-start.1 = (bf16[2,256,128]{2,1,0:T(8,128)(2,1)S(1)}, bf16[2,256,128]{2,1,0:T(8,128)(2,1)S(1)}, u32[]{:S(2)}, u32[]{:S(2)}) collective-permute-start(bf16[2,256,128]{2,1,0:T(8,128)(2,1)S(1)} %pad_maximum_fusion.refs_6_), channel_id=1, source_target_pairs={{0,3},{1,4},{2,5},{3,6},{4,7},{5,8},{6,9},{7,10},{8,11},{9,12},{10... | collective-permute-start | bytes 393224 | tf_op jit(solution)/shard_map/ppermute | solution.py:185
  14.8 9.4 %copy-start.1 = (bf16[2,256,128]{2,1,0:T(8,128)(2,1)}, bf16[2,256,128]{2,1,0:T(8,128)(2,1)S(1)}, u32[]{:S(2)}) copy-start(bf16[2,256,128]{2,1,0:T(8,128)(2,1)S(1)} %collective-permute-done.5.refs_8_) | copy-start | bytes 393220
  14.8 9.4 %collective-permute-start = (bf16[2,256,128]{2,1,0:T(8,128)(2,1)S(1)}, bf16[2,256,128]{2,1,0:T(8,128)(2,1)S(1)}, u32[]{:S(2)}, u32[]{:S(2)}) collective-permute-start(bf16[2,256,128]{2,1,0:T(8,128)(2,1)S(1)} %pad_maximum_fusion.refs_6_), channel_id=1, source_target_pairs={{0,4},{1,5},{2,6},{3,7},{4,8},{5,9},{6,10},{7,11},{8,12},{9,13},{1... | collective-permute-start | bytes 393224 | tf_op jit(solution)/shard_map/ppermute | solution.py:185
  17.9 6.2 %copy-start.2 = (bf16[2,256,128]{2,1,0:T(8,128)(2,1)}, bf16[2,256,128]{2,1,0:T(8,128)(2,1)S(1)}, u32[]{:S(2)}) copy-start(bf16[2,256,128]{2,1,0:T(8,128)(2,1)S(1)} %collective-permute-done.4.refs_7_) | copy-start | bytes 393220
  17.9 6.2 %copy-start.3 = (bf16[2,256,128]{2,1,0:T(8,128)(2,1)}, bf16[2,256,128]{2,1,0:T(8,128)(2,1)S(1)}, u32[]{:S(2)}) copy-start(bf16[2,256,128]{2,1,0:T(8,128)(2,1)S(1)} %collective-permute-done.3.refs_5_) | copy-start | bytes 393220
  19.3 4.9 %copy-start.4 = (bf16[2,256,128]{2,1,0:T(8,128)(2,1)}, bf16[2,256,128]{2,1,0:T(8,128)(2,1)S(1)}, u32[]{:S(2)}) copy-start(bf16[2,256,128]{2,1,0:T(8,128)(2,1)S(1)} %collective-permute-done.2.refs_4_) | copy-start | bytes 393220
  19.3 4.9 %copy-start.5 = (bf16[2,256,128]{2,1,0:T(8,128)(2,1)}, bf16[2,256,128]{2,1,0:T(8,128)(2,1)S(1)}, u32[]{:S(2)}) copy-start(bf16[2,256,128]{2,1,0:T(8,128)(2,1)S(1)} %collective-permute-done.1.refs_3_) | copy-start | bytes 393220
  24.2 0.6 copy-start.6
  38.1 11.3 %collective-permute-start.6 = (bf16[2,256,128]{2,1,0:T(8,128)(2,1)}, bf16[2,256,128]{2,1,0:T(8,128)(2,1)S(1)}, u32[]{:S(2)}, u32[]{:S(2)}) collective-permute-start(bf16[2,256,128]{2,1,0:T(8,128)(2,1)} %get-tuple-element.16), channel_id=1, source_target_pairs={{0,28},{1,29},{2,30},{3,31},{4,0},{5,1},{6,2},{7,3},{8,4},{9,5},{1... | collective-permute-start | bytes 393224 | tf_op jit(solution)/shard_map/ppermute | solution.py:185
  38.2 13.8 %collective-permute-start.7 = (bf16[2,256,128]{2,1,0:T(8,128)(2,1)}, bf16[2,256,128]{2,1,0:T(8,128)(2,1)S(1)}, u32[]{:S(2)}, u32[]{:S(2)}) collective-permute-start(bf16[2,256,128]{2,1,0:T(8,128)(2,1)} %get-tuple-element.17), channel_id=1, source_target_pairs={{0,29},{1,30},{2,31},{3,0},{4,1},{5,2},{6,3},{7,4},{8,5},{9,6},{10... | collective-permute-start | bytes 393224 | tf_op jit(solution)/shard_map/ppermute | solution.py:185
  40.1 11.9 %collective-permute-start.8 = (bf16[2,256,128]{2,1,0:T(8,128)(2,1)}, bf16[2,256,128]{2,1,0:T(8,128)(2,1)S(1)}, u32[]{:S(2)}, u32[]{:S(2)}) collective-permute-start(bf16[2,256,128]{2,1,0:T(8,128)(2,1)} %get-tuple-element.18), channel_id=1, source_target_pairs={{0,30},{1,31},{2,0},{3,1},{4,2},{5,3},{6,4},{7,5},{8,6},{9,7},{10,... | collective-permute-start | bytes 393224 | tf_op jit(solution)/shard_map/ppermute | solution.py:185
  46.5 7.2 %collective-permute-start.9 = (bf16[2,256,128]{2,1,0:T(8,128)(2,1)}, bf16[2,256,128]{2,1,0:T(8,128)(2,1)S(1)}, u32[]{:S(2)}, u32[]{:S(2)}) collective-permute-start(bf16[2,256,128]{2,1,0:T(8,128)(2,1)} %get-tuple-element.19), channel_id=1, source_target_pairs={{0,31},{1,0},{2,1},{3,2},{4,3},{5,4},{6,5},{7,6},{8,7},{9,8},{10,9... | collective-permute-start | bytes 393224 | tf_op jit(solution)/shard_map/ppermute | solution.py:185
  49.4 11.1 %collective-permute-start.10 = (bf16[2,256,128]{2,1,0:T(8,128)(2,1)}, bf16[2,256,128]{2,1,0:T(8,128)(2,1)S(1)}, u32[]{:S(2)}, u32[]{:S(2)}) collective-permute-start(bf16[2,256,128]{2,1,0:T(8,128)(2,1)} %get-tuple-element.20), channel_id=1, source_target_pairs={{0,24},{1,25},{2,26},{3,27},{4,28},{5,29},{6,30},{7,31},{8,0},{9,1... | collective-permute-start | bytes 393224 | tf_op jit(solution)/shard_map/ppermute | solution.py:185
  49.5 14.8 %collective-permute-start.11 = (bf16[2,256,128]{2,1,0:T(8,128)(2,1)}, bf16[2,256,128]{2,1,0:T(8,128)(2,1)S(1)}, u32[]{:S(2)}, u32[]{:S(2)}) collective-permute-start(bf16[2,256,128]{2,1,0:T(8,128)(2,1)} %get-tuple-element.21), channel_id=1, source_target_pairs={{0,16},{1,17},{2,18},{3,19},{4,20},{5,21},{6,22},{7,23},{8,24},{9,... | collective-permute-start | bytes 393224 | tf_op jit(solution)/shard_map/ppermute | solution.py:185

commit v3 on v2

v3 whole, which is shorter than its diff:
```python
import functools

import jax
import jax.numpy as jnp
from jax import lax
from jax.experimental import pallas as pl
from jax.experimental.pallas import tpu as pltpu
from jax.sharding import PartitionSpec as P

BLK = 128
WIN = 1024
FAR = 6
AXES = ("ctxa", "ctxb")
NEG = -1e30
BIG = 1e30
LOG2E = 1.4426950408889634
NT = (((1,), (1,)), ((), ()))
NN = (((1,), (0,)), ((), ()))
RELAY_IN = True
RELAY_OUT = False
BF16, F32 = jnp.bfloat16, jnp.float32


def dot(a, b, dims):
    return lax.dot_general(a, b, dims, preferred_element_type=F32)


class Plan:
    def __init__(self, tok, heads, width, shards, distances):
        self.tok, self.heads, self.width = tok, heads, width
        self.shards, self.distances = shards, distances
        self.per = tok // BLK
        self.rows = BLK * heads
        self.scale = 1.0 / width**0.5
        self.win = WIN // BLK + 1
        self.blocks = self.win + len(distances)
        self.keys = self.blocks * BLK
        self.parts = [self.order(block) for block in range(self.per)]

    def order(self, block):
        groups = {"far": [], "odd": [], "own": [], "even": []}
        for level in range(len(self.distances)):
            groups["far"].append((level, block * BLK, None))
        for part in range(self.win):
            piece, offset = divmod(block + part, self.per)
            behind = self.shards - piece
            if behind == 0:
                groups["own"].append((0, offset * BLK, part))
            elif behind % 2:
                groups["odd"].append((behind // 2, offset * BLK, part))
            else:
                groups["even"].append((behind // 2 - 1, offset * BLK, part))
        return groups

    def flat(self, block):
        return [
            (name,) + entry for name in ("far", "odd", "own", "even") for entry in self.parts[block][name]
        ]

    def span(self, block, name):
        start = 0
        for group in ("far", "odd", "own", "even"):
            size = len(self.parts[block][group]) * BLK
            if group == name:
                return slice(start, start + size)
            start += size


def backward(plan, block, name, refs, grads, dq_ref, start):
    q_ref, g_ref, p_ref, v_ref, kt_ref = refs
    span = plan.span(block, name)
    rows = slice(block * plan.rows, (block + 1) * plan.rows)
    probs = p_ref[block, span, :]
    g_aug = g_ref[rows, :]
    d = (probs.astype(F32) * dot(v_ref[block, span, :], g_aug, NT)).astype(BF16)
    dv = dot(probs, g_aug[:, : plan.width], NN)
    dk = dot(d, q_ref[rows, :], NN) * plan.scale
    dq = dot(kt_ref[block, :, span], d, NN)
    if start:
        dq_ref[block] = dq
    else:
        dq_ref[block] = dq_ref[block] + dq
    for index, (slot, offset, _) in enumerate(plan.parts[block][name]):
        part = slice(index * BLK, (index + 1) * BLK)
        keys = slice(offset, offset + BLK)
        grads[slot, 0, keys, :] += dk[part]
        grads[slot, 1, keys, :] += dv[part]


def forward_kernel(plan, *refs):
    evens, levels = plan.shards // 2, len(plan.distances)
    q_ref, g_ref = refs[:2]
    near_refs = refs[2 : 3 + evens]
    swap_refs = refs[3 + evens : 4 + 2 * evens]
    far_refs = refs[4 + 2 * evens : 4 + 2 * evens + levels]
    rest = refs[4 + 2 * evens + levels :]
    att_ref, p_ref, v_ref, kt_ref, ga_ref, dq_ref = rest[:6]
    farg_refs = rest[6 : 6 + levels]
    odd_c, k_c, vt_c, s_c, grads = rest[6 + levels :]
    width, rows_n, keys_n = plan.width, plan.rows, plan.keys
    device = lax.axis_index(AXES)
    parity = device % 2

    def valid(block, name, slot, part):
        if part is None:
            return device >= plan.distances[slot]
        return device * plan.per + block + part >= plan.win - 1

    for side in range(2):

        @pl.when(parity == side)
        def _():
            for slot in range(evens):
                odd_c[slot] = swap_refs[slot + 1 - side][...]

    lane = lax.broadcasted_iota(jnp.int32, (keys_n, width), 1)
    ones = jnp.where(lane < 3, 1.0, 0.0).astype(BF16)
    key_in = lax.broadcasted_iota(jnp.int32, (BLK, rows_n), 0)
    tok_in = lax.broadcasted_iota(jnp.int32, (BLK, rows_n), 1) // plan.heads
    grads[...] = jnp.zeros_like(grads)
    for block in range(plan.per):
        rows = slice(block * rows_n, (block + 1) * rows_n)
        parts = plan.flat(block)
        v_ref[block, :, width:] = ones
        vt_c[block, width:, :] = jnp.ones((16, keys_n), BF16)
        for index, (name, slot, offset, part) in enumerate(parts):
            held = slice(index * BLK, (index + 1) * BLK)
            if name == "far":
                source = far_refs[slot]
            elif name == "odd":
                source = odd_c.at[slot]
            elif name == "own":
                source = near_refs[0]
            else:
                source = near_refs[slot + 1]
            keys = source[0, offset : offset + BLK, :]
            values = source[1, offset : offset + BLK, :]
            k_c[block, held, :width] = keys
            k_c[block, held, width:] = keys
            v_ref[block, held, :width] = values
            kt_ref[block, :, held] = keys.T
            vt_c[block, :width, held] = values.T
        scaled = q_ref[rows, :].astype(F32) * (plan.scale * LOG2E)
        q_hi = scaled.astype(BF16)
        q_lo = (scaled - q_hi.astype(F32)).astype(BF16)
        s_c[block] = dot(k_c[block], jnp.concatenate([q_hi, q_lo], axis=1), NT)
        top = jnp.full((8, rows_n), NEG, F32)
        for index, (name, slot, offset, part) in enumerate(parts):
            held = slice(index * BLK, (index + 1) * BLK)
            if part == 0:
                s_c[block, held, :] = jnp.where(key_in > tok_in, s_c[block, held, :], NEG)
            if part == plan.win - 1:
                s_c[block, held, :] = jnp.where(key_in <= tok_in, s_c[block, held, :], NEG)
            part_top = jnp.max(s_c[block, held, :].reshape(BLK // 8, 8, rows_n), axis=0)
            top = jnp.maximum(top, jnp.where(valid(block, name, slot, part), part_top, NEG))
        row_max = jnp.max(top, axis=0, keepdims=True)
        for index, (name, slot, offset, part) in enumerate(parts):
            held = slice(index * BLK, (index + 1) * BLK)
            shift = jnp.where(valid(block, name, slot, part), row_max, BIG)
            p_ref[block, held, :] = jnp.exp2(s_c[block, held, :] - shift).astype(BF16)
        acc = dot(vt_c[block], p_ref[block], NN)
        inverse = 1.0 / acc[width : width + 1, :]
        att = (acc[:width, :] * inverse).T.astype(BF16)
        att_ref[rows, :] = att
        spread = jnp.broadcast_to(inverse, (width, rows_n)).T
        g_norm = (g_ref[rows, :].astype(F32) * spread).astype(BF16)
        delta = -jnp.sum(g_norm.astype(F32) * att.astype(F32), axis=1, keepdims=True)
        d_hi = delta.astype(BF16).astype(F32)
        d_mid = (delta - d_hi).astype(BF16).astype(F32)
        d_lo = delta - d_hi - d_mid
        at = lax.broadcasted_iota(jnp.int32, (rows_n, width), 1)
        tail = jnp.where(at == 0, d_hi, jnp.where(at == 1, d_mid, jnp.where(at == 2, d_lo, 0.0)))
        ga_ref[rows, :width] = g_norm
        ga_ref[rows, width:] = tail.astype(BF16)
        backward(plan, block, "far", (q_ref, ga_ref, p_ref, v_ref, kt_ref), grads, dq_ref, True)
    for level in range(levels):
        farg_refs[level][...] = grads[level].astype(BF16)


def odd_kernel(plan, q_ref, ga_ref, p_ref, v_ref, kt_ref, dqi_ref, out_ref, dq_ref, grads):
    grads[...] = jnp.zeros_like(grads)
    dq_ref[...] = dqi_ref[...]
    for block in range(plan.per):
        backward(plan, block, "odd", (q_ref, ga_ref, p_ref, v_ref, kt_ref), grads, dq_ref, False)
    out_ref[...] = grads[...].astype(BF16)


def own_kernel(plan, q_ref, ga_ref, p_ref, v_ref, kt_ref, dqi_ref, out_ref, dq_ref):
    out_ref[...] = jnp.zeros_like(out_ref)
    dq_ref[...] = dqi_ref[...]
    for block in range(plan.per):
        backward(plan, block, "own", (q_ref, ga_ref, p_ref, v_ref, kt_ref), out_ref, dq_ref, False)


def even_kernel(plan, *refs):
    q_ref, ga_ref, p_ref, v_ref, kt_ref, dqi_ref, recv_ref = refs[:7]
    evens = plan.shards // 2
    out_refs, qg_ref = refs[7 : 7 + evens], refs[7 + evens]
    grads, dq_c = refs[8 + evens :]
    parity = lax.axis_index(AXES) % 2
    dq_c[...] = dqi_ref[...]

    @pl.when(parity == 0)
    def _():
        for slot in range(evens):
            if slot + 1 < evens:
                grads[slot] = recv_ref[slot + 1].astype(F32)
            else:
                grads[slot] = jnp.zeros_like(grads[slot])

    @pl.when(parity == 1)
    def _():
        for slot in range(evens):
            grads[slot] = recv_ref[slot].astype(F32)

    for block in range(plan.per):
        backward(plan, block, "even", (q_ref, ga_ref, p_ref, v_ref, kt_ref), grads, dq_c, False)
        rows = slice(block * plan.rows, (block + 1) * plan.rows)
        qg_ref[rows, :] = (dq_c[block] * plan.scale).T.astype(BF16)
    for slot in range(evens):
        out_refs[slot][...] = grads[slot].astype(BF16)


def sum_kernel(count, *refs):
    own_ref, recv_ref = refs[:2]
    term_refs = refs[2 : 2 + count]
    kg_ref, vg_ref = refs[2 + count :]
    keep = (lax.axis_index(AXES) % 2 == 0).astype(F32)
    for index, out_ref in enumerate((kg_ref, vg_ref)):
        total = own_ref[0, index] + recv_ref[0, index].astype(F32) * keep
        for term in term_refs:
            total = total + term[index].astype(F32)
        out_ref[...] = total.astype(BF16)


def call(kernel, outs, args, scratch=(), limit=40, name=None):
    vmem = pl.BlockSpec(memory_space=pltpu.VMEM)
    return pl.pallas_call(
        kernel,
        out_shape=[jax.ShapeDtypeStruct(s, d) if not keep else pltpu.VMEM(s, d) for s, d, keep in outs],
        in_specs=[vmem] * len(args),
        out_specs=[vmem] * len(outs),
        scratch_shapes=list(scratch),
        compiler_params=pltpu.CompilerParams(vmem_limit_bytes=limit << 20),
        name=name,
    )(*args)


def shifted(value, by):
    count = lax.axis_size(AXES)
    return lax.ppermute(value, AXES, [(i, (i + by) % count) for i in range(count)])


def swapped(value):
    return lax.ppermute(value, AXES, [(i, i ^ 1) for i in range(lax.axis_size(AXES))])


def body(queries, key_vectors, value_vectors, out_grad):
    tok, heads, width = queries.shape
    devices_all = lax.axis_size(AXES)
    shards = WIN // tok
    stride = 2 * WIN // tok
    distances = tuple(
        stride * 2**level for level in range(FAR) if stride * 2**level < devices_all
    )
    plan = Plan(tok, heads, width, shards, distances)
    evens, per, keys = shards // 2, plan.per, plan.keys
    paired = jnp.stack([key_vectors, value_vectors])
    near = [paired] + [shifted(paired, 2 * slot + 2) for slot in range(evens)]
    swaps = [swapped(piece) for piece in near]
    far = [shifted(paired, distances[0])]
    for level in range(1, len(distances)):
        if RELAY_IN:
            far.append(shifted(far[-1], distances[level - 1]))
        else:
            far.append(shifted(paired, distances[level]))
    q_rows = queries.reshape(tok * heads, width)
    g_rows = out_grad.reshape(tok * heads, width)
    total_rows = tok * heads
    pair = (2, tok, width)
    outs = call(
        functools.partial(forward_kernel, plan),
        [
            ((total_rows, width), BF16, False),
            ((per, keys, plan.rows), BF16, True),
            ((per, keys, 2 * width), BF16, True),
            ((per, width, keys), BF16, True),
            ((total_rows, 2 * width), BF16, True),
            ((per, width, plan.rows), F32, True),
        ]
        + [(pair, BF16, False)] * len(distances),
        [q_rows, g_rows, *near, *swaps, *far],
        [
            pltpu.VMEM((evens,) + pair, BF16),
            pltpu.VMEM((per, keys, 2 * width), BF16),
            pltpu.VMEM((per, width + 16, keys), BF16),
            pltpu.VMEM((per, keys, plan.rows), F32),
            pltpu.VMEM((len(distances),) + pair, F32),
        ],
        name="forward",
    )
    attention, probs, values, keys_t, g_aug, dq = outs[:6]
    far_terms = list(outs[6:])
    shared = (q_rows, g_aug, probs, values, keys_t)
    dq_shape = ((per, width, plan.rows), F32, True)
    odd_terms, dq = call(
        functools.partial(odd_kernel, plan),
        [((evens,) + pair, BF16, False), dq_shape],
        [*shared, dq],
        [pltpu.VMEM((evens,) + pair, F32)],
        name="odd",
    )
    recv = swapped(odd_terms)
    if RELAY_OUT:
        for level in range(len(distances) - 1, 0, -1):
            far_terms[level - 1] = far_terms[level - 1] + shifted(far_terms[level], -distances[level - 1])
        returned = [shifted(far_terms[0], -distances[0])]
    else:
        returned = [shifted(term, -by) for term, by in zip(far_terms, distances)]
    own_terms, dq = call(
        functools.partial(own_kernel, plan),
        [((1,) + pair, F32, True), dq_shape],
        [*shared, dq],
        name="own",
    )
    outs = call(
        functools.partial(even_kernel, plan),
        [(pair, BF16, False)] * evens + [((total_rows, width), BF16, False)],
        [*shared, dq, recv],
        [pltpu.VMEM((evens,) + pair, F32), pltpu.VMEM((per, width, plan.rows), F32)],
        name="even",
    )
    returned += [shifted(term, -(2 * slot + 2)) for slot, term in enumerate(outs[:evens])]
    key_grad, value_grad = call(
        functools.partial(sum_kernel, len(returned)),
        [((tok, width), BF16, False)] * 2,
        [own_terms, recv, *returned],
        name="total",
    )
    return (
        attention.reshape(queries.shape),
        outs[evens].reshape(queries.shape),
        key_grad,
        value_grad,
    )


def solution(mesh):
    rows = P(AXES, None, None)
    keys = P(AXES, None)
    return jax.shard_map(
        body,
        mesh=mesh,
        in_specs=(rows, keys, keys, rows),
        out_specs=(rows, rows, keys, keys),
        check_vma=False,
    )
```

time: 66.2 us -> 47.2 us (0.71)
  the two profiles are of different devices: /device:TPU:0 before, /device:TPU:5 now
where the time goes in v3:
time: 47.2 us; the launch traced here: 46.9 us
  starting transfers between devices  19 us (40%)
  Pallas kernels  13.4 us (28%)
  waiting for transfers between devices  10.9 us (23%)
  local copies, waits for them, and re-layouts  2.08 us (4%)
  other arithmetic  0.89 us (2%)
  between operations  0.67 us (1%)
    pallas_call x5, Pallas kernels, call(): pl.pallas_call(kernel, out_shape=[jax.ShapeDtypeStruct(s, d) if not keep...  13.4 us
    ppermute x8, waiting for transfers between devices, shifted(): lax.ppermute(value, AXES, [(i, (i + by) % count) for i in range(count)])  10.8 us
    ppermute x8, starting transfers between devices, shifted(): lax.ppermute(value, AXES, [(i, (i + by) % count) for i in range(count)])  10.2 us
    ppermute x4, starting transfers between devices, swapped(): lax.ppermute(value, AXES, [(i, i ^ 1) for i in range(lax.axis_size(AXES))])  8.74 us
    unnamed x4, local copies, waits for them, and re-layouts  2.08 us
  transfers between devices with their start and end apart: 12, of which 5 were waited for; matrix products, arithmetic and copies ran while one was open for 0% of the time, Pallas kernels for 9%

profile of v3, /device:TPU:5, one launch (start us, length us, event | category | flops | bytes accessed | tf_op | source)
XLA Modules:
  0.0 46.9 jit_solution(2869260145605508031)
XLA Ops:
  0.6 0.9 %pad_maximum_fusion.refs_2_ = bf16[2,256,128]{2,1,0:T(8,128)(2,1)S(1)} fusion(bf16[1,256,128]{2,1,0:T(8,128)(2,1)} %bitcast.11, bf16[1,256,128]{2,1,0:T(8,128)(2,1)} %bitcast.12), kind=kLoop, calls=%fused_computation | loop fusion | flops 65536 | bytes 262144 | tf_op jit(solution)/shard_map/stack | solution.py:268
  1.5 1.3 %collective-permute-start.5 = (bf16[2,256,128]{2,1,0:T(8,128)(2,1)S(1)}, bf16[2,256,128]{2,1,0:T(8,128)(2,1)S(1)}, u32[]{:S(2)}, u32[]{:S(2)}) collective-permute-start(bf16[2,256,128]{2,1,0:T(8,128)(2,1)S(1)} %pad_maximum_fusion.refs_2_), channel_id=1, source_target_pairs={{0,8},{1,9},{2,10},{3,11},{4,12},{5,13},{6,14},{7,15},{8,16},{9,17... | collective-permute-start | bytes 393224 | tf_op jit(solution)/shard_map/ppermute | solution.py:251
  2.9 1.2 %collective-permute-start.1 = (bf16[2,256,128]{2,1,0:T(8,128)(2,1)S(1)}, bf16[2,256,128]{2,1,0:T(8,128)(2,1)S(1)}, u32[]{:S(2)}, u32[]{:S(2)}) collective-permute-start(bf16[2,256,128]{2,1,0:T(8,128)(2,1)S(1)} %pad_maximum_fusion.refs_2_), channel_id=1, source_target_pairs={{0,4},{1,5},{2,6},{3,7},{4,8},{5,9},{6,10},{7,11},{8,12},{9,13},{1... | collective-permute-start | bytes 393224 | tf_op jit(solution)/shard_map/ppermute | solution.py:251
  4.1 1.2 %collective-permute-start = (bf16[2,256,128]{2,1,0:T(8,128)(2,1)S(1)}, bf16[2,256,128]{2,1,0:T(8,128)(2,1)S(1)}, u32[]{:S(2)}, u32[]{:S(2)}) collective-permute-start(bf16[2,256,128]{2,1,0:T(8,128)(2,1)S(1)} %pad_maximum_fusion.refs_2_), channel_id=1, source_target_pairs={{0,2},{1,3},{2,4},{3,5},{4,6},{5,7},{6,8},{7,9},{8,10},{9,11},{10,... | collective-permute-start | bytes 393224 | tf_op jit(solution)/shard_map/ppermute | solution.py:251
  5.3 1.5 %collective-permute-start.2 = (bf16[2,256,128]{2,1,0:T(8,128)(2,1)S(1)}, bf16[2,256,128]{2,1,0:T(8,128)(2,1)S(1)}, u32[]{:S(2)}, u32[]{:S(2)}) collective-permute-start(bf16[2,256,128]{2,1,0:T(8,128)(2,1)S(1)} %pad_maximum_fusion.refs_2_), channel_id=1, source_target_pairs={{0,1},{1,0},{2,3},{3,2},{4,5},{5,4},{6,7},{7,6},{8,9},{9,8},{10,11... | collective-permute-start | bytes 393224 | tf_op jit(solution)/shard_map/ppermute | solution.py:255
  6.8 1.0 %collective-permute-done.5.refs_8_ = bf16[2,256,128]{2,1,0:T(8,128)(2,1)S(1)} collective-permute-done((bf16[2,256,128]{2,1,0:T(8,128)(2,1)S(1)}, bf16[2,256,128]{2,1,0:T(8,128)(2,1)S(1)}, u32[]{:S(2)}, u32[]{:S(2)}) %collective-permute-start.5) | collective-permute-done | bytes 131104 | tf_op jit(solution)/shard_map/ppermute | solution.py:251
  7.9 0.3 collective-permute-start.6
  8.1 0.0 collective-permute-done.1.refs_4_
  8.1 3.5 %collective-permute-start.4 = (bf16[2,256,128]{2,1,0:T(8,128)(2,1)S(1)}, bf16[2,256,128]{2,1,0:T(8,128)(2,1)S(1)}, u32[]{:S(2)}, u32[]{:S(2)}) collective-permute-start(bf16[2,256,128]{2,1,0:T(8,128)(2,1)S(1)} %collective-permute-done.1.refs_4_), channel_id=1, source_target_pairs={{0,1},{1,0},{2,3},{3,2},{4,5},{5,4},{6,7},{7,6},{8,9},{9,8},{10,11... | collective-permute-start | bytes 393224 | tf_op jit(solution)/shard_map/ppermute | solution.py:255
  11.6 0.0 collective-permute-start.3
  11.6 1.9 %collective-permute-done.6.refs_9_ = bf16[2,256,128]{2,1,0:T(8,128)(2,1)S(1)} collective-permute-done((bf16[2,256,128]{2,1,0:T(8,128)(2,1)S(1)}, bf16[2,256,128]{2,1,0:T(8,128)(2,1)S(1)}, u32[]{:S(2)}, u32[]{:S(2)}) %collective-permute-start.6) | collective-permute-done | bytes 131104 | tf_op jit(solution)/shard_map/ppermute | solution.py:251
  13.5 1.0 %copy-done = bf16[256,8,128]{2,1,0:T(8,128)(2,1)S(1)} copy-done((bf16[256,8,128]{2,1,0:T(8,128)(2,1)S(1)}, bf16[256,8,128]{2,1,0:T(8,128)(2,1)}, u32[]{:S(2)}) %copy-start) | copy-done | bytes 524312
  14.5 1.0 %copy-done.1 = bf16[256,8,128]{2,1,0:T(8,128)(2,1)S(1)} copy-done((bf16[256,8,128]{2,1,0:T(8,128)(2,1)S(1)}, bf16[256,8,128]{2,1,0:T(8,128)(2,1)}, u32[]{:S(2)}) %copy-start.1) | copy-done | bytes 524312
  15.6 6.5 %forward.1 = (bf16[2048,128]{1,0:T(8,128)(2,1)}, bf16[2,1408,1024]{2,1,0:T(8,128)(2,1)S(1)}, bf16[2,1408,256]{2,1,0:T(8,128)(2,1)S(1)}, bf16[2,128,1408]{2,1,0:T...) custom-call(bf16[2048,128]{1,0:T(8,128)(2,1)S(1)} %bitcast.6, ...), custom_call_target="tpu_custom_call" | custom-call | tf_op jit(solution)/shard_map/forward/pallas_call | solution.py:238
  22.1 2.2 %odd.1 = (bf16[2,2,256,128]{3,2,1,0:T(8,128)(2,1)S(1)}, f32[2,128,1024]{2,1,0:T(8,128)S(1)}) custom-call(bf16[2048,128]{1,0:T(8,128)(2,1)S(1)} %bitcast.7, bf16[2048,256]{1,0:T(8,128)(2,1)S(1)} %get-tuple-element.22.ga_ref.refs_1_, bf16[2,1408,1024]{2,1,0:T(8,128)(2,1)S(1)} %get-tuple-element.23.p_ref.refs_2_, ...), custom_call_target="tpu_custom_call" | custom-call | tf_op jit(solution)/shard_map/odd/pallas_call | solution.py:238
  24.3 3.8 %collective-permute-start.7 = (bf16[2,2,256,128]{3,2,1,0:T(8,128)(2,1)S(1)}, bf16[2,2,256,128]{3,2,1,0:T(8,128)(2,1)S(1)}, u32[]{:S(2)}, u32[]{:S(2)}) collective-permute-start(bf16[2,2,256,128]{3,2,1,0:T(8,128)(2,1)S(1)} %get-tuple-element.29), channel_id=1, source_target_pairs={{0,1},{1,0},{2,3},{3,2},{4,5},{5,4},{6,7},{7,6},{8,9},{9,8},{10,11... | collective-permute-start | bytes 786440 | tf_op jit(solution)/shard_map/ppermute | solution.py:255
  28.0 1.1 %own.1 = (f32[1,2,256,128]{3,2,1,0:T(8,128)S(1)}, f32[2,128,1024]{2,1,0:T(8,128)S(1)}) custom-call(bf16[2048,128]{1,0:T(8,128)(2,1)S(1)} %bitcast.8, bf16[2048,256]{1,0:T(8,128)(2,1)S(1)} %get-tuple-element.22.ga_ref.refs_1_, bf16[2,1408,1024]{2,1,0:T(8,128)(2,1)S(1)} %get-tuple-element.23.p_ref.refs_2_, ...), custom_call_target="tpu_custom_call" | custom-call | tf_op jit(solution)/shard_map/own/pallas_call | solution.py:238
  29.1 0.1 collective-permute-done.7.refs_6_.refs_1_
  29.2 2.9 %even.1 = (bf16[2,256,128]{2,1,0:T(8,128)(2,1)S(1)}, bf16[2,256,128]{2,1,0:T(8,128)(2,1)S(1)}, bf16[2048,128]{1,0:T(8,128)(2,1)}) custom-call(bf16[2048,128]{1,0:T(8,128)(2,1)S(1)} %bitcast.9, bf16[2048,256]{1,0:T(8,128)(2,1)S(1)} %get-tuple-element.22.ga_ref.refs_1_, bf16[2,1408,1024]{2,1,0:T(8,128)(2,1)S(1)} %get-tuple-element.23.p_ref.refs_2_, ...), custom_call_target="tpu_custom_call" | custom-call | tf_op jit(solution)/shard_map/even/pallas_call | solution.py:238
  32.1 1.1 %collective-permute-start.10 = (bf16[2,256,128]{2,1,0:T(8,128)(2,1)S(1)}, bf16[2,256,128]{2,1,0:T(8,128)(2,1)S(1)}, u32[]{:S(2)}, u32[]{:S(2)}) collective-permute-start(bf16[2,256,128]{2,1,0:T(8,128)(2,1)S(1)} %get-tuple-element.34), channel_id=1, source_target_pairs={{0,30},{1,31},{2,0},{3,1},{4,2},{5,3},{6,4},{7,5},{8,6},{9,7},{10,... | collective-permute-start | bytes 393224 | tf_op jit(solution)/shard_map/ppermute | solution.py:251
  33.2 5.0 %collective-permute-start.11 = (bf16[2,256,128]{2,1,0:T(8,128)(2,1)S(1)}, bf16[2,256,128]{2,1,0:T(8,128)(2,1)S(1)}, u32[]{:S(2)}, u32[]{:S(2)}) collective-permute-start(bf16[2,256,128]{2,1,0:T(8,128)(2,1)S(1)} %get-tuple-element.35), channel_id=1, source_target_pairs={{0,28},{1,29},{2,30},{3,31},{4,0},{5,1},{6,2},{7,3},{8,4},{9,5},{1... | collective-permute-start | bytes 393224 | tf_op jit(solution)/shard_map/ppermute | solution.py:251
  38.3 0.5 %collective-permute-done.10.refs_4_ = bf16[2,256,128]{2,1,0:T(8,128)(2,1)S(1)} collective-permute-done((bf16[2,256,128]{2,1,0:T(8,128)(2,1)S(1)}, bf16[2,256,128]{2,1,0:T(8,128)(2,1)S(1)}, u32[]{:S(2)}, u32[]{:S(2)}) %collective-permute-start.10) | collective-permute-done | bytes 131104 | tf_op jit(solution)/shard_map/ppermute | solution.py:251
  38.8 7.3 %collective-permute-done.11.refs_5_ = bf16[2,256,128]{2,1,0:T(8,128)(2,1)S(1)} collective-permute-done((bf16[2,256,128]{2,1,0:T(8,128)(2,1)S(1)}, bf16[2,256,128]{2,1,0:T(8,128)(2,1)S(1)}, u32[]{:S(2)}, u32[]{:S(2)}) %collective-permute-start.11) | collective-permute-done | bytes 131104 | tf_op jit(solution)/shard_map/ppermute | solution.py:251
  46.2 0.7 %total.1 = (bf16[256,128]{1,0:T(8,128)(2,1)}, bf16[256,128]{1,0:T(8,128)(2,1)}) custom-call(f32[1,2,256,128]{3,2,1,0:T(8,128)S(1)} %get-tuple-element.31.refs_0_, bf16[2,2,256,128]{3,2,1,0:T(8,128)(2,1)S(1)} %collective-permute-done.7.refs_6_.refs_1_, bf16[2,256,128]{2,1,0:T(8,128)(2,1)S(1)} %collective-permute-done.8.refs_2_, ...), custom_call_target="tpu_custom_call" | custom-call | tf_op jit(solution)/shard_map/total/pallas_call | solution.py:238
  (10 shorter events, 0.0 us)
Async XLA Ops:
  1.5 6.4 %collective-permute-start.5 = (bf16[2,256,128]{2,1,0:T(8,128)(2,1)S(1)}, bf16[2,256,128]{2,1,0:T(8,128)(2,1)S(1)}, u32[]{:S(2)}, u32[]{:S(2)}) collective-permute-start(bf16[2,256,128]{2,1,0:T(8,128)(2,1)S(1)} %pad_maximum_fusion.refs_2_), channel_id=1, source_target_pairs={{0,8},{1,9},{2,10},{3,11},{4,12},{5,13},{6,14},{7,15},{8,16},{9,17... | collective-permute-start | bytes 393224 | tf_op jit(solution)/shard_map/ppermute | solution.py:251
  2.9 5.3 %collective-permute-start.1 = (bf16[2,256,128]{2,1,0:T(8,128)(2,1)S(1)}, bf16[2,256,128]{2,1,0:T(8,128)(2,1)S(1)}, u32[]{:S(2)}, u32[]{:S(2)}) collective-permute-start(bf16[2,256,128]{2,1,0:T(8,128)(2,1)S(1)} %pad_maximum_fusion.refs_2_), channel_id=1, source_target_pairs={{0,4},{1,5},{2,6},{3,7},{4,8},{5,9},{6,10},{7,11},{8,12},{9,13},{1... | collective-permute-start | bytes 393224 | tf_op jit(solution)/shard_map/ppermute | solution.py:251
  4.1 7.5 %collective-permute-start = (bf16[2,256,128]{2,1,0:T(8,128)(2,1)S(1)}, bf16[2,256,128]{2,1,0:T(8,128)(2,1)S(1)}, u32[]{:S(2)}, u32[]{:S(2)}) collective-permute-start(bf16[2,256,128]{2,1,0:T(8,128)(2,1)S(1)} %pad_maximum_fusion.refs_2_), channel_id=1, source_target_pairs={{0,2},{1,3},{2,4},{3,5},{4,6},{5,7},{6,8},{7,9},{8,10},{9,11},{10,... | collective-permute-start | bytes 393224 | tf_op jit(solution)/shard_map/ppermute | solution.py:251
  5.3 6.3 %collective-permute-start.2 = (bf16[2,256,128]{2,1,0:T(8,128)(2,1)S(1)}, bf16[2,256,128]{2,1,0:T(8,128)(2,1)S(1)}, u32[]{:S(2)}, u32[]{:S(2)}) collective-permute-start(bf16[2,256,128]{2,1,0:T(8,128)(2,1)S(1)} %pad_maximum_fusion.refs_2_), channel_id=1, source_target_pairs={{0,1},{1,0},{2,3},{3,2},{4,5},{5,4},{6,7},{7,6},{8,9},{9,8},{10,11... | collective-permute-start | bytes 393224 | tf_op jit(solution)/shard_map/ppermute | solution.py:255
  7.9 5.6 %collective-permute-start.6 = (bf16[2,256,128]{2,1,0:T(8,128)(2,1)S(1)}, bf16[2,256,128]{2,1,0:T(8,128)(2,1)S(1)}, u32[]{:S(2)}, u32[]{:S(2)}) collective-permute-start(bf16[2,256,128]{2,1,0:T(8,128)(2,1)S(1)} %collective-permute-done.5.refs_8_), channel_id=1, source_target_pairs={{0,8},{1,9},{2,10},{3,11},{4,12},{5,13},{6,14},{7,15},{8,16},{9,17... | collective-permute-start | bytes 393224 | tf_op jit(solution)/shard_map/ppermute | solution.py:251
  8.1 5.4 %collective-permute-start.4 = (bf16[2,256,128]{2,1,0:T(8,128)(2,1)S(1)}, bf16[2,256,128]{2,1,0:T(8,128)(2,1)S(1)}, u32[]{:S(2)}, u32[]{:S(2)}) collective-permute-start(bf16[2,256,128]{2,1,0:T(8,128)(2,1)S(1)} %collective-permute-done.1.refs_4_), channel_id=1, source_target_pairs={{0,1},{1,0},{2,3},{3,2},{4,5},{5,4},{6,7},{7,6},{8,9},{9,8},{10,11... | collective-permute-start | bytes 393224 | tf_op jit(solution)/shard_map/ppermute | solution.py:255
  11.6 1.9 %collective-permute-start.3 = (bf16[2,256,128]{2,1,0:T(8,128)(2,1)S(1)}, bf16[2,256,128]{2,1,0:T(8,128)(2,1)S(1)}, u32[]{:S(2)}, u32[]{:S(2)}) collective-permute-start(bf16[2,256,128]{2,1,0:T(8,128)(2,1)S(1)} %collective-permute-done.refs_3_), channel_id=1, source_target_pairs={{0,1},{1,0},{2,3},{3,2},{4,5},{5,4},{6,7},{7,6},{8,9},{9,8},{10,11... | collective-permute-start | bytes 393224 | tf_op jit(solution)/shard_map/ppermute | solution.py:255
  13.5 1.0 %copy-start = (bf16[256,8,128]{2,1,0:T(8,128)(2,1)S(1)}, bf16[256,8,128]{2,1,0:T(8,128)(2,1)}, u32[]{:S(2)}) copy-start(bf16[256,8,128]{2,1,0:T(8,128)(2,1)} %param.4) | copy-start | bytes 1572868
  14.5 1.0 %copy-start.1 = (bf16[256,8,128]{2,1,0:T(8,128)(2,1)S(1)}, bf16[256,8,128]{2,1,0:T(8,128)(2,1)}, u32[]{:S(2)}) copy-start(bf16[256,8,128]{2,1,0:T(8,128)(2,1)} %param.7) | copy-start | bytes 1572868
  24.3 4.9 %collective-permute-start.7 = (bf16[2,2,256,128]{3,2,1,0:T(8,128)(2,1)S(1)}, bf16[2,2,256,128]{3,2,1,0:T(8,128)(2,1)S(1)}, u32[]{:S(2)}, u32[]{:S(2)}) collective-permute-start(bf16[2,2,256,128]{3,2,1,0:T(8,128)(2,1)S(1)} %get-tuple-element.29), channel_id=1, source_target_pairs={{0,1},{1,0},{2,3},{3,2},{4,5},{5,4},{6,7},{7,6},{8,9},{9,8},{10,11... | collective-permute-start | bytes 786440 | tf_op jit(solution)/shard_map/ppermute | solution.py:255
  28.0 10.3 %collective-permute-start.8 = (bf16[2,256,128]{2,1,0:T(8,128)(2,1)S(1)}, bf16[2,256,128]{2,1,0:T(8,128)(2,1)S(1)}, u32[]{:S(2)}, u32[]{:S(2)}) collective-permute-start(bf16[2,256,128]{2,1,0:T(8,128)(2,1)S(1)} %get-tuple-element.32), channel_id=1, source_target_pairs={{0,24},{1,25},{2,26},{3,27},{4,28},{5,29},{6,30},{7,31},{8,0},{9,1... | collective-permute-start | bytes 393224 | tf_op jit(solution)/shard_map/ppermute | solution.py:251
  28.0 10.3 %collective-permute-start.9 = (bf16[2,256,128]{2,1,0:T(8,128)(2,1)S(1)}, bf16[2,256,128]{2,1,0:T(8,128)(2,1)S(1)}, u32[]{:S(2)}, u32[]{:S(2)}) collective-permute-start(bf16[2,256,128]{2,1,0:T(8,128)(2,1)S(1)} %get-tuple-element.33), channel_id=1, source_target_pairs={{0,16},{1,17},{2,18},{3,19},{4,20},{5,21},{6,22},{7,23},{8,24},{9,... | collective-permute-start | bytes 393224 | tf_op jit(solution)/shard_map/ppermute | solution.py:251
  32.1 6.7 %collective-permute-start.10 = (bf16[2,256,128]{2,1,0:T(8,128)(2,1)S(1)}, bf16[2,256,128]{2,1,0:T(8,128)(2,1)S(1)}, u32[]{:S(2)}, u32[]{:S(2)}) collective-permute-start(bf16[2,256,128]{2,1,0:T(8,128)(2,1)S(1)} %get-tuple-element.34), channel_id=1, source_target_pairs={{0,30},{1,31},{2,0},{3,1},{4,2},{5,3},{6,4},{7,5},{8,6},{9,7},{10,... | collective-permute-start | bytes 393224 | tf_op jit(solution)/shard_map/ppermute | solution.py:251
  33.2 12.9 %collective-permute-start.11 = (bf16[2,256,128]{2,1,0:T(8,128)(2,1)S(1)}, bf16[2,256,128]{2,1,0:T(8,128)(2,1)S(1)}, u32[]{:S(2)}, u32[]{:S(2)}) collective-permute-start(bf16[2,256,128]{2,1,0:T(8,128)(2,1)S(1)} %get-tuple-element.35), channel_id=1, source_target_pairs={{0,28},{1,29},{2,30},{3,31},{4,0},{5,1},{6,2},{7,3},{8,4},{9,5},{1... | collective-permute-start | bytes 393224 | tf_op jit(solution)/shard_map/ppermute | solution.py:251
